TPU v7x, 32 devices: a whole 2x2x4 slice. The times are simulated.
32 devices in a mesh: ctx: 16 (over z, x, core), fsdp: 2 (over y).
Axes of the slice: x: 2, y: 2, z: 4, core: 2. Of those that a mesh axis runs over, the one named last changes fastest.
Arguments:
- hidden_in: bfloat16 [2, 2048, 1024], P('fsdp', 'ctx'), may hold values from -6 to 6
- doc_lengths: int32 [2, 8], P('fsdp'), may hold values from 1 to 1920, as said below
- attn_gain: float32 [1024], replicated, may hold values from 0.5 to 1.5
- query_gain: float32 [64], replicated, may hold values from 0.5 to 1.5
- key_norm_gain: float32 [64], replicated, may hold values from 0.5 to 1.5
- ffn_gain: float32 [1024], replicated, may hold values from 0.5 to 1.5
- query_proj: float32 [1024, 1024], P('fsdp'), may hold values from -0.1875 to 0.1875
- key_weight: float32 [1024, 512], P('fsdp'), may hold values from -0.1875 to 0.1875
- value_weight: float32 [1024, 512], P('fsdp'), may hold values from -0.1875 to 0.1875
- attn_proj: float32 [1024, 1024], P('fsdp'), may hold values from -3 to 3
- gate_proj: float32 [1024, 4608], P('fsdp'), may hold values from -0.1875 to 0.1875
- up_proj: float32 [1024, 4608], P('fsdp'), may hold values from -0.1875 to 0.1875
- down_proj: float32 [4608, 1024], P('fsdp'), may hold values from -0.09375 to 0.09375
- out_cotangent: bfloat16 [2, 2048, 1024], P('fsdp', 'ctx'), may hold values from -6 to 6
Outputs:
- hidden_out: float32 [2, 2048, 1024], P('fsdp', 'ctx')
- input_grad: float32 [2, 2048, 1024], P('fsdp', 'ctx')
- attn_gain_grad: float32 [1024], replicated
- query_gain_grad: float32 [64], replicated
- key_gain_grad: float32 [64], replicated
- ffn_gain_grad: float32 [1024], replicated
- query_grad: float32 [1024, 1024], P('fsdp', 'ctx')
- key_grad: float32 [1024, 512], P('fsdp', 'ctx')
- value_grad: float32 [1024, 512], P('fsdp', 'ctx')
- attn_grad: float32 [1024, 1024], P('fsdp', 'ctx')
- gate_grad: float32 [1024, 4608], P('fsdp', 'ctx')
- up_grad: float32 [1024, 4608], P('fsdp', 'ctx')
- down_grad: float32 [4608, 1024], P('fsdp', 'ctx')
Inputs may be any that keep to these rules, and one draw needn't show every extreme that they name: `doc_lengths`: each stream's 8 document lengths sum to 2048; in every stream exactly one document has 1920 tokens, and it is neither the first nor the last of its stream.
All inputs are finite; a program needn't handle non-finite values.
Results may differ from a plain program's by a relative error of at most 0.014.
Values may be sent and summed in bfloat16 or wider, within the bound.
A program may use at most 320 MiB of HBM per device.

v0:
```python
import functools
import math

import jax
import jax.numpy as jnp
from jax import lax
from jax.experimental import pallas as pl
from jax.experimental.pallas import tpu as pltpu
from jax.sharding import PartitionSpec as P

QUERY_HEADS = 16
KEY_VALUE_HEADS = 8
HEAD_SIZE = 64
FF = 4608
WIDTH = 1024
ROWS = 128

epsilon = 1e-05
rope_base = 1000000.0
MESH = pl.DeviceIdType.MESH
ANY = pl.ANY
bf16 = jnp.bfloat16
f32 = jnp.float32


def who():
    n = lax.axis_size("ctx")
    c = lax.axis_index("ctx")
    f = lax.axis_index("fsdp")
    q = n // 4
    return c // q, (c % q) // 2, c % 2, f


def dev(z, m, core, f):
    return (z * (lax.axis_size("ctx") // 4) + m * 2 + core, f)


def slot(z, core):
    return z * 2 + core


def enter(peers):
    bar = pltpu.get_barrier_semaphore()
    for p in peers:
        pl.semaphore_signal(bar, inc=1, device_id=p, device_id_type=MESH)
    pl.semaphore_wait(bar, len(peers))


def rcopy(src, dst, s, r, to):
    return pltpu.make_async_remote_copy(
        src_ref=src, dst_ref=dst, send_sem=s, recv_sem=r, device_id=to, device_id_type=MESH
    )


def comm_params(cid):
    return pltpu.CompilerParams(collective_id=cid, has_side_effects=True)


def any_specs(n):
    return [pl.BlockSpec(memory_space=ANY)] * n


def gather8_kernel(x_ref, o_ref, ss, rs, ls):
    z, m, core, f = who()
    sib = dev(z, m, 1 - core, f)
    peers = [dev((z + s) % 4, m, core, f) for s in (1, 2, 3)]
    me = slot(z, core)
    own = pltpu.make_async_copy(x_ref, o_ref.at[me], ls)
    own.start()
    enter([sib] + peers)
    first = []
    for k in (1, 0, 2):
        cp = rcopy(x_ref, o_ref.at[me], ss.at[k], rs.at[k], peers[k])
        cp.start()
        first.append((k, cp))
    cp0 = rcopy(x_ref, o_ref.at[me], ss.at[3], rs.at[3], sib)
    cp0.start()
    fw = []
    for k, cp in first:
        sl = slot((z + 3 - k) % 4, core)
        cp.wait_recv()
        cp = rcopy(o_ref.at[sl], o_ref.at[sl], ss.at[4 + k], rs.at[4 + k], sib)
        cp.start()
        fw.append(cp)
    for cp in fw + [cp0]:
        cp.wait_recv()
    for cp in [cp for _, cp in first] + [cp0] + fw:
        cp.wait_send()
    own.wait()


def gather8(x, cid):
    return pl.pallas_call(
        gather8_kernel,
        out_shape=jax.ShapeDtypeStruct((8,) + x.shape, x.dtype),
        in_specs=any_specs(1),
        out_specs=any_specs(1)[0],
        scratch_shapes=[
            pltpu.SemaphoreType.DMA((7,)),
            pltpu.SemaphoreType.DMA((7,)),
            pltpu.SemaphoreType.DMA,
        ],
        compiler_params=comm_params(cid),
        name="gather8_%d" % cid,
    )(x)


def across_kernel(both, same, x_ref, o_ref, ss, rs, ls):
    z, m, core, f = who()
    M = lax.axis_size("ctx") // 8
    count = M * 2 if both else M
    me = m * 2 + f if both else m
    others = [(me + s) % count for s in range(1, count)]
    peers = [dev(z, o // 2, core, o % 2) if both else dev(z, o, core, f) for o in others]

    def src(k):
        return x_ref if same else x_ref.at[k]

    own = pltpu.make_async_copy(src(me), o_ref.at[me], ls)
    own.start()
    enter(peers)
    cps = []
    for s in range(count - 1):
        cp = rcopy(src(others[s]), o_ref.at[me], ss.at[s], rs.at[s], peers[s])
        cp.start()
        cps.append(cp)
    for cp in cps:
        cp.wait_recv()
    for cp in cps:
        cp.wait_send()
    own.wait()


def across(x, both, same, cid):
    shp = x.shape if same else x.shape[1:]
    count = lax.axis_size("ctx") // (4 if both else 8)
    return pl.pallas_call(
        functools.partial(across_kernel, both, same),
        out_shape=jax.ShapeDtypeStruct((count,) + shp, x.dtype),
        in_specs=any_specs(1),
        out_specs=any_specs(1)[0],
        scratch_shapes=[
            pltpu.SemaphoreType.DMA((count - 1,)),
            pltpu.SemaphoreType.DMA((count - 1,)),
            pltpu.SemaphoreType.DMA,
        ],
        compiler_params=comm_params(cid),
        name="across_%d" % cid,
    )(x)


def scatter8_kernel(x_ref, o_ref, a, b, s_buf, d, ls, s1, r1, s2, r2):
    z, m, core, f = who()
    sib = dev(z, m, 1 - core, f)
    to = [(z + s) % 4 for s in (1, 2, 3, 0)]
    peers = [dev(zz, m, core, f) for zz in to[:3]]
    loads = []
    for k in range(4):
        cp = pltpu.make_async_copy(x_ref.at[slot(to[k], core)], a.at[k], ls.at[k])
        cp.start()
        loads.append(cp)
    enter([sib] + peers)
    ones = []
    for k in range(4):
        cp = rcopy(x_ref.at[slot(to[k], 1 - core)], b.at[k], s1.at[k], r1.at[k], sib)
        cp.start()
        ones.append(cp)
    twos = []
    for k in range(3):
        loads[k].wait()
        ones[k].wait_recv()
        s_buf[k] = (a[k].astype(f32) + b[k].astype(f32)).astype(s_buf.dtype)
        cp = rcopy(s_buf.at[k], d.at[k], s2.at[k], r2.at[k], peers[k])
        cp.start()
        twos.append(cp)
    loads[3].wait()
    ones[3].wait_recv()
    total = a[3].astype(f32) + b[3].astype(f32)
    for k in range(3):
        twos[k].wait_recv()
        total = total + d[k].astype(f32)
    o_ref[...] = total
    for cp in ones + twos:
        cp.wait_send()


def scatter8(x, cid):
    shp = x.shape[1:]
    return pl.pallas_call(
        scatter8_kernel,
        out_shape=jax.ShapeDtypeStruct(shp, f32),
        in_specs=any_specs(1),
        out_specs=pl.BlockSpec(memory_space=pltpu.VMEM),
        scratch_shapes=[
            pltpu.VMEM((4,) + shp, x.dtype),
            pltpu.VMEM((4,) + shp, x.dtype),
            pltpu.VMEM((3,) + shp, x.dtype),
            pltpu.VMEM((3,) + shp, x.dtype),
            pltpu.SemaphoreType.DMA((4,)),
            pltpu.SemaphoreType.DMA((4,)),
            pltpu.SemaphoreType.DMA((4,)),
            pltpu.SemaphoreType.DMA((3,)),
            pltpu.SemaphoreType.DMA((3,)),
        ],
        compiler_params=comm_params(cid),
        name="scatter8_%d" % cid,
    )(x)


def back_product(left, right):
    return lax.dot_general(
        left, right, (((1,), (1,)), ((), ())), preferred_element_type=f32
    )


def lead_sum(left, right):
    return lax.dot_general(
        left, right, (((0,), (0,)), ((), ())), preferred_element_type=f32
    )


def dot(left, right):
    return jnp.dot(left, right, preferred_element_type=f32)


BLOCK = 2 * ROWS


def block_weights(q, k, begin, z, m, mm, span):
    keys = (z + 1) * BLOCK
    key = lax.broadcasted_iota(jnp.int32, (1, keys), 1)
    key = key // BLOCK * span + key % BLOCK + mm * BLOCK
    token = z * span + m * BLOCK + lax.broadcasted_iota(jnp.int32, (BLOCK, 1), 0)
    e = jnp.exp(back_product(q, k))
    return jnp.where((key >= begin) & (key <= token), e, 0.0)


def attend_kernel(span, m_ref, q_ref, kv_ref, begin_ref, sum_ref, tot_ref):
    m = m_ref[0]
    for z in range(4):
        rows = slice(z * BLOCK, (z + 1) * BLOCK)
        keys = (z + 1) * BLOCK
        for h in range(2):
            lanes = slice(h * 64, h * 64 + 64)
            acc = jnp.zeros((BLOCK, 64), f32)
            tot = jnp.zeros((BLOCK, 1), f32)
            q = q_ref[rows, lanes]

            def step(mm, carry):
                acc, tot = carry
                e = block_weights(q, kv_ref[mm, :keys, :64], begin_ref[rows, :], z, m, mm, span)
                acc = acc + dot(e.astype(bf16), kv_ref[mm, :keys, 64:])
                return acc, tot + jnp.sum(e, axis=1, keepdims=True)

            acc, tot = lax.fori_loop(0, kv_ref.shape[0], step, (acc, tot))
            sum_ref[rows, lanes] = acc
            tot_ref[rows, lanes] = jnp.broadcast_to(tot, (BLOCK, 64))


VM = pltpu.VMEM


def vspecs(n):
    return [pl.BlockSpec(memory_space=VM)] * n


def attend(m, q, kv, begin, span):
    n = q.shape[0]
    return pl.pallas_call(
        functools.partial(attend_kernel, span),
        out_shape=(jax.ShapeDtypeStruct((n, 128), f32), jax.ShapeDtypeStruct((n, 128), f32)),
        in_specs=[pl.BlockSpec(memory_space=pltpu.SMEM)] + vspecs(3),
        out_specs=tuple(vspecs(2)),
        cost_estimate=pl.CostEstimate(flops=2**31, bytes_accessed=2**22, transcendentals=2**22),
        compiler_params=pltpu.CompilerParams(vmem_limit_bytes=40 * 2**20),
        name="attend",
    )(m, q, kv, begin)


def attend_back_kernel(span, m_ref, q_ref, kv_ref, begin_ref, g_ref, delta_ref, dq_ref, dkv_ref, acc_ref):
    m = m_ref[0]
    dq_ref[...] = jnp.zeros_like(dq_ref)

    def step(mm, _):
        acc_ref[...] = jnp.zeros_like(acc_ref)
        for z in range(4):
            rows = slice(z * BLOCK, (z + 1) * BLOCK)
            keys = (z + 1) * BLOCK
            for h in range(2):
                lanes = slice(h * 64, h * 64 + 64)
                q = q_ref[rows, lanes]
                g = g_ref[rows, lanes]
                k = kv_ref[mm, :keys, :64]
                v = kv_ref[mm, :keys, 64:]
                e = block_weights(q, k, begin_ref[rows, :], z, m, mm, span)
                dp = back_product(g, v)
                ds = (e * (dp - delta_ref[rows, h * 64 : h * 64 + 1])).astype(bf16)
                dq_ref[rows, lanes] += dot(ds, k)
                acc_ref[:keys, :64] += lead_sum(ds, q)
                acc_ref[:keys, 64:] += lead_sum(e.astype(bf16), g)
        dkv_ref[mm] = acc_ref[...].astype(dkv_ref.dtype)
        return 0

    lax.fori_loop(0, kv_ref.shape[0], step, 0)


def attend_back(m, q, kv, begin, g, delta, span):
    n = q.shape[0]
    return pl.pallas_call(
        functools.partial(attend_back_kernel, span),
        out_shape=(jax.ShapeDtypeStruct((n, 128), f32), jax.ShapeDtypeStruct(kv.shape, bf16)),
        in_specs=[pl.BlockSpec(memory_space=pltpu.SMEM)] + vspecs(5),
        out_specs=tuple(vspecs(2)),
        scratch_shapes=[pltpu.VMEM((n, 128), f32)],
        cost_estimate=pl.CostEstimate(flops=2**33, bytes_accessed=2**23, transcendentals=2**22),
        compiler_params=pltpu.CompilerParams(vmem_limit_bytes=48 * 2**20),
        name="attend_back",
    )(m, q, kv, begin, g, delta)


def begin_of(token, doc_ref):
    begin = jnp.zeros(token.shape, jnp.int32)
    start = doc_ref[0, 0]
    for d in range(1, doc_ref.shape[1]):
        begin = jnp.where(token >= start, start, begin)
        start = start + doc_ref[0, d]
    return begin


def turn(v):
    lane = lax.broadcasted_iota(jnp.int32, v.shape, 1)
    n = v.shape[1]
    return jnp.where(lane % 64 < 32, pltpu.roll(v, n - 32, 1), pltpu.roll(v, 32, 1))


def head_scale(v):
    sq = v * v
    if v.shape[1] == 64:
        return lax.rsqrt(jnp.mean(sq, axis=1, keepdims=True) + epsilon)
    low = lax.broadcasted_iota(jnp.int32, v.shape, 1) < 64
    a = jnp.sum(jnp.where(low, sq, 0.0), axis=1, keepdims=True)
    b = jnp.sum(jnp.where(low, 0.0, sq), axis=1, keepdims=True)
    return lax.rsqrt(jnp.where(low, a, b) * (1.0 / 64) + epsilon)


def front_kernel(
    doc_ref, x_ref, c_hbm, wh_ref, wg_hbm, wu_hbm, wd_hbm, wo_hbm, again_ref, qgain_ref, kgain_ref,
    x_all, c_all, w_heads, w_gate, w_up, w_down, w_out, q_rows, kv_all, att, summed, totals,
    stacked, normed, cosine, sine,
    s_x, r_x, s_c, r_c, s_h, r_h, s_w, r_w, s_v, r_v, s_o, r_o, s_k, r_k, l_s,
):
    z, m, core, f = who()
    M = lax.axis_size("ctx") // 8
    span = lax.axis_size("ctx") // 4 * ROWS
    half_width = WIDTH // 2
    sib = dev(z, m, 1 - core, f)
    zpeers = [dev((z + s) % 4, m, core, f) for s in (1, 2, 3)]
    hm = m % 2
    pair = dev(z, m, core, 1 - f)
    beside = dev(z, m + 1 - 2 * hm, core, f)
    mpeers = [dev(z, (m + s) % M, core, f) for s in range(1, M)]
    me = slot(z, core)
    owner = f == z // 2

    stay = [
        pltpu.make_async_copy(c_hbm, c_all.at[me], l_s.at[0]),
        pltpu.make_async_copy(wg_hbm, w_gate.at[pl.ds(f * half_width, half_width)], l_s.at[1]),
        pltpu.make_async_copy(wu_hbm, w_up.at[pl.ds(f * half_width, half_width)], l_s.at[2]),
        pltpu.make_async_copy(wo_hbm, w_out.at[pl.ds(f * half_width, half_width)], l_s.at[3]),
    ]
    for cp in stay:
        cp.start()
    stay_down = pltpu.make_async_copy(wd_hbm, w_down, l_s.at[4])

    @pl.when(owner)
    def _():
        stay_down.start()

    enter([sib, pair] + zpeers + mpeers)

    def gather(src, dst, ss, rs, k):
        if k < 3:
            return rcopy(src, dst.at[me], ss.at[k], rs.at[k], zpeers[k])
        if k == 3:
            return rcopy(src, dst.at[me], ss.at[k], rs.at[k], sib)
        j = slot((z + 3 - (k - 4)) % 4, core)
        return rcopy(dst.at[j], dst.at[j], ss.at[k], rs.at[k], sib)

    def x_copy(k):
        return gather(x_ref, x_all, s_x, r_x, k)

    def c_copy(k):
        return gather(c_hbm, c_all, s_c, r_c, k)

    for k in (1, 0, 2, 3):
        x_copy(k).start()
    head_rows = pl.ds(f * half_width, half_width)
    heads_copy = rcopy(wh_ref, w_heads.at[head_rows], s_h.at[0], r_h.at[0], pair)
    heads_copy.start()

    quarter = half_width // 2
    eighth = half_width // 4
    cols = wd_hbm.shape[0]

    def w_copy(k, stage):
        src, dst = ((wg_hbm, w_gate), (wu_hbm, w_up), (wd_hbm, w_down), (wo_hbm, w_out))[k]
        base = 0 if k == 2 else (f if stage == 0 else 1 - f) * half_width
        size = (quarter, quarter, cols // 2, eighth)[k]
        part = hm * 2 + core if k == 3 else hm
        place = dst.at[pl.ds(pl.multiple_of(base + part * size, 8), size)]
        if stage == 0:
            here = src.at[pl.ds(pl.multiple_of(part * size, 8), size)]
            return rcopy(here, place, s_w.at[k], r_w.at[k], pair)
        return rcopy(place, place, s_v.at[k], r_v.at[k], beside)

    def out_copy(k):
        part = (hm if k == 0 else 1 - hm) * 2 + core
        base = (1 - f) * half_width
        place = w_out.at[pl.ds(pl.multiple_of(base + part * eighth, 8), eighth)]
        return rcopy(place, place, s_o.at[k], r_o.at[k], sib)

    for k in (0, 1, 3):
        w_copy(k, 0).start()

    @pl.when(owner)
    def _():
        w_copy(2, 0).start()

    w_heads[head_rows] = wh_ref[...]
    x_all[me] = x_ref[...]

    lane = lax.broadcasted_iota(jnp.int32, (1, 128), 1) % 32
    freq = jnp.exp(lane.astype(f32) * (-2.0 / 64 * math.log(rope_base)))
    sign = jnp.where(lax.broadcasted_iota(jnp.int32, (1, 128), 1) % 64 < 32, -1.0, 1.0)

    def tokens_of(zz):
        return zz * span + m * BLOCK + lax.broadcasted_iota(jnp.int32, (BLOCK, 1), 0)

    def table(zz, _):
        rows = pl.ds(pl.multiple_of(zz * BLOCK, BLOCK), BLOCK)
        token = tokens_of(zz)
        place = (token - begin_of(token, doc_ref)).astype(f32)
        angle = place * freq
        cosine[rows, :] = jnp.cos(angle)
        sine[rows, :] = jnp.sin(angle) * sign
        return 0

    lax.fori_loop(0, 4, table, 0)
    for k in range(3):
        x_copy(k).wait_recv()
        x_copy(k + 4).start()
    for k in (1, 0, 2, 3):
        c_copy(k).start()
    heads_copy.wait_recv()

    def kv_copy(b, s):
        rows = pl.ds(pl.multiple_of(b * BLOCK, BLOCK), BLOCK)
        place = kv_all.at[m, rows]
        return rcopy(place, place, s_k.at[b, s], r_k.at[b, s], mpeers[s])

    again = again_ref[...]
    qgain = qgain_ref[...]
    kgain = kgain_ref[...]

    for k in range(3, 7):
        x_copy(k).wait_recv()

    def project(b, _):
        rows = pl.ds(pl.multiple_of(b * BLOCK, BLOCK), BLOCK)
        x = jnp.concatenate([x_all[2 * b], x_all[2 * b + 1]], axis=0).astype(f32)
        nb = (
            x * lax.rsqrt(jnp.mean(x * x, axis=-1, keepdims=True) + epsilon) * again
        ).astype(bf16)
        normed[rows, :] = nb
        st = dot(nb, w_heads[...])
        stacked[rows, :] = st
        co = cosine[rows, :]
        si = sine[rows, :]
        q = st[:, :128]
        q = q * head_scale(q) * qgain
        q_rows[rows, :] = ((q * co + turn(q) * si) * HEAD_SIZE ** (-0.5)).astype(bf16)
        kv = st[:, 128:]
        low = lax.broadcasted_iota(jnp.int32, kv.shape, 1) < 64
        k = kv * head_scale(kv) * kgain
        kv_all[m, rows, :] = jnp.where(low, k * co + turn(k) * si, kv).astype(bf16)
        for s in range(M - 1):
            kv_copy(b, s).start()
        return 0

    lax.fori_loop(0, 4, project, 0)
    for k in range(2):
        w_copy(k, 0).wait_recv()
        w_copy(k, 1).start()

    summed[...] = jnp.zeros_like(summed)
    totals[...] = jnp.zeros_like(totals)

    def attend(s, _):
        mm = (m + M - s) % M

        @pl.when(s > 0)
        def _():
            for b in range(4):
                rows = pl.ds(b * BLOCK, BLOCK)
                place = kv_all.at[mm, rows]
                rcopy(place, place, s_k.at[b, s - 1], r_k.at[b, s - 1], sib).wait_recv()

        for zz in range(4):
            rows = slice(zz * BLOCK, (zz + 1) * BLOCK)
            keys = (zz + 1) * BLOCK
            begin = begin_of(tokens_of(zz), doc_ref)
            for h in range(2):
                lanes = slice(h * 64, h * 64 + 64)
                e = block_weights(
                    q_rows[rows, lanes], kv_all[mm, :keys, :64], begin, zz, m, mm, span
                )
                summed[rows, lanes] += dot(e.astype(bf16), kv_all[mm, :keys, 64:])
                totals[rows, lanes] += jnp.broadcast_to(
                    jnp.sum(e, axis=1, keepdims=True), (BLOCK, 64)
                )
        return 0

    lax.fori_loop(0, M, attend, 0)
    for b in range(4):
        rows = slice(b * BLOCK, (b + 1) * BLOCK)
        att[b] = (summed[rows, :] / totals[rows, :]).astype(bf16)

    w_copy(3, 0).wait_recv()
    w_copy(3, 1).start()
    out_copy(0).start()

    @pl.when(jnp.logical_not(owner))
    def _():
        w_copy(2, 0).wait_recv()
        w_copy(2, 1).start()

    for k in range(3):
        c_copy(k).wait_recv()
        c_copy(k + 4).start()

    def w_got(k):
        dst = (w_gate, w_up, w_down, w_out)[k]
        base = 0 if k == 2 else (1 - f) * half_width
        size = (quarter, quarter, cols // 2, eighth)[k]
        part = (1 - hm) * 2 + core if k == 3 else 1 - hm
        place = dst.at[pl.ds(pl.multiple_of(base + part * size, 8), size)]
        return rcopy(place, place, s_v.at[k], r_v.at[k], beside)

    w_got(3).wait_recv()
    out_copy(1).start()
    for k in range(2):
        w_got(k).wait_recv()

    @pl.when(jnp.logical_not(owner))
    def _():
        w_got(2).wait_recv()
        w_copy(2, 1).wait_send()

    @pl.when(owner)
    def _():
        stay_down.wait()
        w_copy(2, 0).wait_send()

    for k in range(3, 7):
        c_copy(k).wait_recv()
    for k in range(2):
        out_copy(k).wait_recv()
    for cp in stay:
        cp.wait()
    heads_copy.wait_send()
    for k in range(7):
        x_copy(k).wait_send()
        c_copy(k).wait_send()
    for k in (0, 1, 3):
        w_copy(k, 0).wait_send()
        w_copy(k, 1).wait_send()
    for k in range(2):
        out_copy(k).wait_send()
    for b in range(4):
        for s in range(M - 1):
            kv_copy(b, s).wait_send()


def front(docs, x, c, wh, wg, wu, wd, wo, again, qgain, kgain, cid):
    n = lax.axis_size("ctx")
    M = n // 8
    cols = FF // 8
    tokens = 8 * ROWS
    sem = pltpu.SemaphoreType.DMA
    shape = jax.ShapeDtypeStruct
    return pl.pallas_call(
        front_kernel,
        out_shape=(
            shape((8, ROWS, WIDTH), bf16),
            shape((8, ROWS, WIDTH), bf16),
            shape((WIDTH, 256), bf16),
            shape((WIDTH, cols), bf16),
            shape((WIDTH, cols), bf16),
            shape((cols, WIDTH), bf16),
            shape((WIDTH, WIDTH), bf16),
            shape((tokens, 128), bf16),
            shape((M, tokens, 128), bf16),
            shape((4, BLOCK, 128), bf16),
            shape((tokens, 128), f32),
            shape((tokens, 128), f32),
            shape((tokens, 256), f32),
            shape((tokens, WIDTH), bf16),
            shape((tokens, 128), f32),
            shape((tokens, 128), f32),
        ),
        in_specs=[pl.BlockSpec(memory_space=pltpu.SMEM)]
        + vspecs(1) + any_specs(1) + vspecs(1) + any_specs(4) + vspecs(3),
        out_specs=tuple(vspecs(1) + any_specs(1) + vspecs(1) + any_specs(4) + vspecs(9)),
        scratch_shapes=[
            sem((7,)), sem((7,)), sem((7,)), sem((7,)), sem((1,)), sem((1,)),
            sem((4,)), sem((4,)), sem((4,)), sem((4,)), sem((2,)), sem((2,)),
            sem((4, M - 1)), sem((4, M - 1)), sem((5,)),
        ],
        compiler_params=pltpu.CompilerParams(
            collective_id=cid, has_side_effects=True, vmem_limit_bytes=60 * 2**20
        ),
        name="front",
    )(docs, x, c, wh, wg, wu, wd, wo, again, qgain, kgain)


def ffn_kernel(
    att_ref, x_hbm, c_hbm, own_c_ref, wo_hbm, wg_hbm, wu_hbm, wd_hbm, gain_ref,
    att_all, branch_ref, gmid_ref, mid_ref, dpart_ref, gpart_ref, glu_rx, down_rx,
    x_v, c_v, wo_v, wg_v, wu_v, wd_v, normed, hid, gg, gu, mid_b, p_out, p_sib, p_sum, p_rx,
    glu_tx, down_tx, br_own,
    ld, s_att, r_att, s_sib, r_sib, s_rs, r_rs, s_br, r_br, s_x, r_x, l_x,
):
    z, m, core, f = who()
    M = lax.axis_size("ctx") // 8
    T = 2 * M
    seg = glu_tx.shape[2]
    each = WIDTH // lax.axis_size("ctx")
    half_width = WIDTH // 2
    sib = dev(z, m, 1 - core, f)
    zs = [(z + s) % 4 for s in (1, 2, 3)]
    zpeers = [dev(zz, m, core, f) for zz in zs]
    group = m * 2 + f
    others = [(group + s) % T for s in range(1, T)]
    tpeers = [dev(z, o // 2, core, o % 2) for o in others]

    loads = []
    for k, (a, b) in enumerate(
        ((wo_hbm, wo_v), (x_hbm, x_v), (wg_hbm, wg_v), (wu_hbm, wu_v), (c_hbm, c_v), (wd_hbm, wd_v))
    ):
        cp = pltpu.make_async_copy(a, b, ld.at[k])
        cp.start()
        loads.append(cp)
    enter([sib] + zpeers + tpeers)

    def lanes(j):
        return pl.ds(pl.multiple_of(j * 128, 128), 128)

    me = slot(z, core)

    def send_att(s, i):
        b = (zs[s] + 1 + i) % 4
        return rcopy(
            att_ref.at[b], att_all.at[b, :, lanes(me)], s_att.at[s, i], r_att.at[s, i], zpeers[s]
        )

    def got_att(s, i):
        b = (z + 1 + i) % 4
        j = slot((z + 3 - s) % 4, core)
        return rcopy(
            att_ref.at[b], att_all.at[b, :, lanes(j)], s_att.at[s, i], r_att.at[s, i], zpeers[s]
        )

    def sib_att(k, i):
        b = (z + 1 + i) % 4
        j = me if k == 3 else slot((z + 3 - k) % 4, core)
        src = att_ref.at[b] if k == 3 else att_all.at[b, :, lanes(j)]
        return rcopy(src, att_all.at[b, :, lanes(j)], s_sib.at[k, i], r_sib.at[k, i], sib)

    def from_sib(k, i):
        b = (z + 1 + i) % 4
        j = slot(z, 1 - core) if k == 3 else slot((z + 3 - k) % 4, 1 - core)
        return rcopy(att_ref.at[b], att_all.at[b, :, lanes(j)], s_sib.at[k, i], r_sib.at[k, i], sib)

    for i in range(4):
        for s in (1, 0, 2):
            send_att(s, i).start()
        sib_att(3, i).start()
    for b in range(4):
        att_all[b, :, lanes(me)] = att_ref[b]

    def forward(i):
        for s in range(3):
            got_att(s, i).wait_recv()
            sib_att(s, i).start()

    def p_copy(i):
        return rcopy(p_out.at[i, 1 - core], p_sib.at[i], s_rs.at[i], r_rs.at[i], sib)

    def rs_copy(i):
        return rcopy(p_sum.at[i], p_rx.at[i], s_rs.at[4 + i], r_rs.at[4 + i], zpeers[i])

    def reduce_block(i):
        p_copy(i).wait_recv()
        p_sum[i] = (p_out[i, core].astype(f32) + p_sib[i].astype(f32)).astype(bf16)
        rs_copy(i).start()

    forward(0)
    gain = gain_ref[...]
    for cp in loads:
        cp.wait()
    for i in range(4):
        b = (z + 1 + i) % 4
        for k in range(4):
            from_sib(k, i).wait_recv()
        mid = x_v[b].astype(f32) + dot(att_all[b], wo_v[...])
        nb = (
            mid * lax.rsqrt(jnp.mean(mid * mid, axis=-1, keepdims=True) + epsilon) * gain
        ).astype(bf16)
        normed[b] = nb
        if i == 3:
            mid_b[0] = mid[:ROWS]
            mid_b[1] = mid[ROWS:]
        if i < 3:
            forward(i + 1)
        gate = dot(nb, wg_v[...])
        up = dot(nb, wu_v[...])
        sig = 1.0 / (1.0 + jnp.exp(-gate))
        silu = gate * sig
        hb = (silu * up).astype(bf16)
        hid[b] = hb
        gh = back_product(c_v[b], wd_v[...])
        ggb = (gh * up * (sig * (1.0 + gate * (1.0 - sig)))).astype(bf16)
        gub = (gh * silu).astype(bf16)
        gg[b] = ggb
        gu[b] = gub
        pb = (back_product(ggb, wg_v[...]) + back_product(gub, wu_v[...])).astype(bf16)
        p_out[i, 0] = pb[:ROWS]
        p_out[i, 1] = pb[ROWS:]
        p_copy(i).start()
        if i > 0:
            reduce_block(i - 1)
        db = dot(hb, wd_v[...]).astype(bf16)
        dpart_ref[b, 0] = db[:ROWS]
        dpart_ref[b, 1] = db[ROWS:]

    def x_copy(which, s):
        tx, rx = (glu_tx, glu_rx) if which < 2 else (down_tx, down_rx)
        if which < 2:
            src, dst = tx.at[others[s], which], rx.at[group, which]
        else:
            src, dst = tx.at[others[s]], rx.at[group]
        return rcopy(src, dst, s_x.at[which, s], r_x.at[which, s], tpeers[s])

    def x_own(which):
        if which < 2:
            return pltpu.make_async_copy(
                glu_tx.at[group, which], glu_rx.at[group, which], l_x.at[which]
            )
        return pltpu.make_async_copy(down_tx.at[group], down_rx.at[group], l_x.at[which])

    def flat(ref):
        return ref[...].reshape(8 * ROWS, ref.shape[-1])

    def glu_grads(which):
        prod = lead_sum(flat((gg, gu)[which]), flat(normed)).astype(bf16)
        for mm in range(M):
            for ff in range(2):
                glu_tx[mm * 2 + ff, which] = prod[
                    mm * seg : (mm + 1) * seg, ff * half_width : (ff + 1) * half_width
                ]
        for s in range(T - 1):
            x_copy(which, s).start()
        x_own(which).start()

    def down_grads():
        prod = lead_sum(flat(hid), flat(c_v))
        for mm in range(M):
            for ff in range(2):
                down_tx[mm * 2 + ff] = jnp.concatenate(
                    [
                        prod[:, blk * each : (blk + 1) * each]
                        for zl in range(2)
                        for cc in range(2)
                        for blk in [(2 * ff + zl) * 2 * M + mm * 2 + cc]
                    ],
                    axis=1,
                ).astype(bf16)
        for s in range(T - 1):
            x_copy(2, s).start()
        x_own(2).start()

    glu_grads(0)

    p_copy(3).wait_recv()
    dy = p_out[3, core].astype(f32) + p_sib[3].astype(f32)
    for i in range(3):
        rs_copy(i).wait_recv()
        dy = dy + p_rx[i].astype(f32)
    mid = mid_b[core]
    r = lax.rsqrt(jnp.mean(mid * mid, axis=-1, keepdims=True) + epsilon)
    gdy = gain * dy
    dv = r * gdy - mid * (r * r * r) * jnp.mean(mid * gdy, axis=-1, keepdims=True)
    gmid = own_c_ref[...].astype(f32) + dv
    gmid_ref[...] = gmid
    mid_ref[...] = mid
    gpart_ref[...] = jnp.sum(dy * mid * r, axis=0, keepdims=True)
    br_own[...] = gmid.astype(bf16)
    branch_ref[me] = br_own[...]

    def br_copy(k):
        if k < 3:
            return rcopy(br_own, branch_ref.at[me], s_br.at[k], r_br.at[k], zpeers[k])
        j = me if k == 3 else slot((z + 3 - (k - 4)) % 4, core)
        return rcopy(
            br_own if k == 3 else branch_ref.at[j], branch_ref.at[j], s_br.at[k], r_br.at[k], sib
        )

    for k in (1, 0, 2, 3):
        br_copy(k).start()
    glu_grads(1)
    down_grads()
    for k in range(3):
        br_copy(k).wait_recv()
        br_copy(k + 4).start()
    for k in range(3, 7):
        br_copy(k).wait_recv()
    for which in range(3):
        x_own(which).wait()
        for s in range(T - 1):
            x_copy(which, s).wait_recv()
    for i in range(4):
        for s in range(3):
            send_att(s, i).wait_send()
        for k in range(4):
            sib_att(k, i).wait_send()
        p_copy(i).wait_send()
    for i in range(3):
        rs_copy(i).wait_send()
    for k in range(7):
        br_copy(k).wait_send()
    for which in range(3):
        for s in range(T - 1):
            x_copy(which, s).wait_send()


def feed_forward(att, x_all, c_all, own_c, w_out, w_gate, w_up, w_down, gain, cid):
    n = lax.axis_size("ctx")
    T, seg, each = n // 4, FF // n, WIDTH // n
    cols = FF // 8
    half_width = WIDTH // 2
    VS, sem = pltpu.VMEM, pltpu.SemaphoreType.DMA
    shape = jax.ShapeDtypeStruct
    return pl.pallas_call(
        ffn_kernel,
        out_shape=(
            shape((4, BLOCK, WIDTH), bf16),
            shape((8, ROWS, WIDTH), bf16),
            shape((ROWS, WIDTH), f32),
            shape((ROWS, WIDTH), f32),
            shape((4, 2, ROWS, WIDTH), bf16),
            shape((1, WIDTH), f32),
            shape((T, 2, seg, half_width), bf16),
            shape((T, cols, 4 * each), bf16),
        ),
        in_specs=vspecs(1) + any_specs(2) + vspecs(1) + any_specs(4) + vspecs(1),
        out_specs=tuple(vspecs(8)),
        scratch_shapes=[
            VS((4, BLOCK, WIDTH), bf16),
            VS((4, BLOCK, WIDTH), bf16),
            VS((WIDTH, WIDTH), bf16),
            VS((WIDTH, cols), bf16),
            VS((WIDTH, cols), bf16),
            VS((cols, WIDTH), bf16),
            VS((4, BLOCK, WIDTH), bf16),
            VS((4, BLOCK, cols), bf16),
            VS((4, BLOCK, cols), bf16),
            VS((4, BLOCK, cols), bf16),
            VS((2, ROWS, WIDTH), f32),
            VS((4, 2, ROWS, WIDTH), bf16),
            VS((4, ROWS, WIDTH), bf16),
            VS((3, ROWS, WIDTH), bf16),
            VS((3, ROWS, WIDTH), bf16),
            VS((T, 2, seg, half_width), bf16),
            VS((T, cols, 4 * each), bf16),
            VS((ROWS, WIDTH), bf16),
            sem((6,)),
            sem((3, 4)),
            sem((3, 4)),
            sem((4, 4)),
            sem((4, 4)),
            sem((7,)),
            sem((7,)),
            sem((7,)),
            sem((7,)),
            sem((3, T - 1)),
            sem((3, T - 1)),
            sem((3,)),
        ],
        compiler_params=pltpu.CompilerParams(
            collective_id=cid, has_side_effects=True, vmem_limit_bytes=60 * 2**20
        ),
        name="feed_forward",
    )(att, x_all, c_all, own_c, w_out, w_gate, w_up, w_down, gain)


def root_mean_norm(rows, gain):
    return (
        rows * lax.rsqrt(jnp.mean(rows * rows, axis=-1, keepdims=True) + epsilon) * gain
    )


def rotary(rows, cosine, sine):
    halfway = rows.shape[-1] // 2
    leading = rows[..., :halfway]
    trailing = rows[..., halfway:]
    return jnp.concatenate(
        [leading * cosine - trailing * sine, leading * sine + trailing * cosine], axis=-1
    )


SWAP = [(0, 1), (1, 0)]


def halves(f, own, other, axis):
    return jnp.where(
        f == 0,
        jnp.concatenate([own, other], axis=axis),
        jnp.concatenate([other, own], axis=axis),
    )


def local(
    hidden_in,
    doc_lengths,
    attn_gain,
    query_gain,
    key_norm_gain,
    ffn_gain,
    query_proj,
    key_weight,
    value_weight,
    attn_proj,
    gate_proj,
    up_proj,
    down_proj,
    out_cotangent,
):
    n_ctx = lax.axis_size("ctx")
    M = n_ctx // 8
    T = 2 * M
    z, m, core, f = who()
    head = slot(z, core)
    tokens = 8 * ROWS
    span = n_ctx // 4 * ROWS
    segment = FF // n_ctx
    columns = M * segment
    half_width = WIDTH // 2
    each = WIDTH // n_ctx

    heads_own = jnp.concatenate(
        [
            lax.dynamic_slice(query_proj, (0, head * 128), (half_width, 128)),
            lax.dynamic_slice(key_weight, (0, head * 64), (half_width, 64)),
            lax.dynamic_slice(value_weight, (0, head * 64), (half_width, 64)),
        ],
        axis=1,
    ).astype(bf16)
    first = z * (n_ctx // 4) + core
    gate_own, up_own = [
        jnp.concatenate(
            [
                lax.dynamic_slice(w, (0, (first + 2 * mm) * segment), (half_width, segment))
                for mm in range(M)
            ],
            axis=1,
        ).astype(bf16)
        for w in (gate_proj, up_proj)
    ]
    down_own = jnp.concatenate(
        [
            lax.dynamic_slice(
                down_proj, ((first + 2 * mm) * segment - f * (FF // 2), 0), (segment, WIDTH)
            )
            for mm in range(M)
        ],
        axis=0,
    ).astype(bf16)
    out_own = attn_proj.astype(bf16)

    cotangent = out_cotangent[0]
    (
        x_rows, c_rows, w_heads, w_gate, w_up, w_down, w_out, q_rows, kv_all, att_own, summed, totals,
        stacked, normed, cos_table, sin_table,
    ) = front(
        doc_lengths,
        hidden_in[0],
        cotangent,
        heads_own,
        gate_own,
        up_own,
        down_own,
        out_own,
        attn_gain[None],
        jnp.tile(query_gain, 2)[None],
        jnp.concatenate([key_norm_gain, jnp.ones((64,), f32)])[None],
        1,
    )
    starts = jnp.cumsum(doc_lengths[0]) - doc_lengths[0]
    token_index = (
        jnp.arange(4, dtype=jnp.int32)[:, None] * span
        + m * BLOCK
        + jnp.arange(BLOCK, dtype=jnp.int32)[None, :]
    ).reshape(tokens, 1)
    after = token_index >= starts[None, :]
    begins = jnp.max(jnp.where(after, starts[None, :], 0), axis=1, keepdims=True)
    cosine = cos_table[:, None, :32]
    sine = sin_table[:, None, 32:64]

    def rotate(q_in, k_in, q_gain, k_gain):
        q_out = (
            rotary(root_mean_norm(q_in.reshape(tokens, 2, HEAD_SIZE), q_gain), cosine, sine)
            * HEAD_SIZE ** (-0.5)
        )
        k_out = rotary(root_mean_norm(k_in.reshape(tokens, 1, HEAD_SIZE), k_gain), cosine, sine)
        return q_out.reshape(tokens, 128), k_out.reshape(tokens, 64)

    _, heads_back = jax.vjp(
        rotate, stacked[:, :128], stacked[:, 128:192], query_gain, key_norm_gain
    )
    m_arr = jnp.full((1,), m, jnp.int32)
    attended, branch, grad_middle, own, down_parts, ffn_gain_part, glu_got, down_got = feed_forward(
        att_own,
        x_rows.reshape(4, BLOCK, WIDTH),
        c_rows.reshape(4, BLOCK, WIDTH),
        cotangent,
        w_out,
        w_gate,
        w_up,
        w_down,
        ffn_gain[None],
        4,
    )
    attended = attended.reshape(tokens, WIDTH)
    branch = branch.reshape(tokens, WIDTH)
    ffn_gain_part = ffn_gain_part[0]
    output = own + scatter8(down_parts.reshape(8, ROWS, WIDTH), 5)

    w_out_head = lax.dynamic_slice(w_out, (head * 128, 0), (128, WIDTH))
    grad_mixed = back_product(branch, w_out_head)
    grad_summed = (grad_mixed / totals).astype(bf16)
    weighted = (grad_mixed * summed / (totals * totals)).reshape(tokens, 2, 64)
    delta = jnp.broadcast_to(
        jnp.sum(weighted, axis=2, keepdims=True), (tokens, 2, 64)
    ).reshape(tokens, 128)
    grad_q, dkv = attend_back(m_arr, q_rows, kv_all, begins, grad_summed, delta, span)
    dkv = jnp.sum(across(dkv, False, False, 6).astype(f32), axis=0)
    gq_pre, gk_pre, q_gain_part, k_gain_part = heads_back((grad_q, dkv[:, :64]))
    grad_stacked = jnp.concatenate([gq_pre, gk_pre, dkv[:, 64:]], axis=1).astype(bf16)
    part_normed = back_product(grad_stacked, w_heads).reshape(8, ROWS, WIDTH).astype(bf16)
    grad_normed = scatter8(part_normed, 7)
    _, attn_back = jax.vjp(root_mean_norm, hidden_in[0].astype(f32), attn_gain)
    grad_resid, attn_gain_part = attn_back(grad_normed)
    input_grad = grad_middle + grad_resid

    glu_grad = jnp.sum(glu_got.astype(f32), axis=0)
    down_sum = jnp.sum(down_got.astype(f32), axis=0)
    gate_grad = jnp.transpose(glu_grad[0])
    up_grad = jnp.transpose(glu_grad[1])

    devices = [
        (zz, mm, cc, ff) for zz in range(4) for mm in range(M) for cc in range(2) for ff in range(2)
    ]

    def number(zz, mm, cc, ff):
        return (zz * (n_ctx // 4) + mm * 2 + cc) * 2 + ff

    down_pieces = down_sum.reshape(columns, 2, 2, each)
    rounds = []
    for dz in range(2):
        for dc in range(2):
            piece = lax.dynamic_slice(
                down_pieces, (0, (z + dz) % 2, (core + dc) % 2, 0), (columns, 1, 1, each)
            ).reshape(columns, each)
            perm = [
                (number(zz, mm, cc, ff), number(2 * ff + (zz + dz) % 2, mm, (cc + dc) % 2, zz // 2))
                for zz, mm, cc, ff in devices
            ]
            rounds.append(lax.ppermute(piece, ("ctx", "fsdp"), perm))
    rounds = jnp.stack(rounds).reshape(2, 2, columns, each)
    rounds = jnp.where(z % 2 == 0, rounds, rounds[::-1])
    rounds = jnp.where(core == 0, rounds, rounds[:, ::-1])
    down_grad = jnp.transpose(
        rounds.reshape(2, 2, M, segment, each), (0, 2, 1, 3, 4)
    ).reshape(FF // 2, each)

    branch_columns = lax.dynamic_slice(
        branch.reshape(tokens, 4, M, 2, each), (0, z, 0, core, 0), (tokens, 1, M, 1, each)
    ).reshape(tokens, M * each)
    attn_part = lead_sum(attended, branch_columns).astype(bf16)
    attn_part = jnp.transpose(
        attn_part.reshape(2, half_width, M, each), (2, 0, 1, 3)
    ).reshape(T, half_width, each)
    attn_grad = jnp.sum(across(attn_part, True, False, 11).astype(f32), axis=0)

    heads_part = lead_sum(normed, grad_stacked).astype(bf16)
    qw, kw = 128 // M, 64 // M
    heads_part = jnp.concatenate(
        [
            heads_part[:, :128].reshape(2, half_width, M, qw),
            heads_part[:, 128:192].reshape(2, half_width, M, kw),
            heads_part[:, 192:].reshape(2, half_width, M, kw),
        ],
        axis=3,
    )
    heads_part = jnp.transpose(heads_part, (2, 0, 1, 3)).reshape(T, half_width, 256 // M)
    heads_grad = jnp.sum(across(heads_part, True, False, 12).astype(f32), axis=0)
    perm = [
        (number(zz, mm, cc, ff), number(zz, (cc * M + mm) // 2, (cc * M + mm) % 2, ff))
        for zz, mm, cc, ff in devices
    ]
    heads_grad = lax.ppermute(heads_grad, ("ctx", "fsdp"), perm)
    query_grad = heads_grad[:, :qw]
    key_grad = heads_grad[:, qw : qw + kw]
    value_grad = heads_grad[:, qw + kw :]

    gains = jnp.concatenate([attn_gain_part, ffn_gain_part, q_gain_part, k_gain_part])
    gains = jnp.sum(gather8(gains.reshape(17, 128), 13), axis=0)
    gains = jnp.sum(across(gains, True, True, 14), axis=0).reshape(-1)
    return (
        output[None],
        input_grad[None],
        gains[:WIDTH],
        gains[2 * WIDTH : 2 * WIDTH + 64],
        gains[2 * WIDTH + 64 :],
        gains[WIDTH : 2 * WIDTH],
        query_grad,
        key_grad,
        value_grad,
        attn_grad,
        gate_grad,
        up_grad,
        down_grad,
    )


def solution(mesh):
    in_specs = (
        P("fsdp", "ctx", None),
        P("fsdp", None),
        P(),
        P(),
        P(),
        P(),
        P("fsdp", None),
        P("fsdp", None),
        P("fsdp", None),
        P("fsdp", None),
        P("fsdp", None),
        P("fsdp", None),
        P("fsdp", None),
        P("fsdp", "ctx", None),
    )
    out_specs = (
        P("fsdp", "ctx", None),
        P("fsdp", "ctx", None),
        P(),
        P(),
        P(),
        P(),
        P("fsdp", "ctx"),
        P("fsdp", "ctx"),
        P("fsdp", "ctx"),
        P("fsdp", "ctx"),
        P("fsdp", "ctx"),
        P("fsdp", "ctx"),
        P("fsdp", "ctx"),
    )
    return jax.shard_map(local, mesh=mesh, in_specs=in_specs, out_specs=out_specs, check_vma=False)
```

profile of v0, /device:TPU:13, one launch (start us, length us, event | category | flops | bytes accessed | tf_op | source)
XLA Modules:
  0.0 402.0 jit_solution(7786370417471851322)
XLA Ops:
  0.8 2.9 convert_element_type.40.wo_hbm
  4.8 1.8 dynamic-slice_convert_fusion.1
  6.6 1.1 pad_maximum_fusion.wd_hbm
  7.7 2.8 dynamic-slice_convert_fusion.3
  10.5 1.1 pad_maximum_fusion.2.wu_hbm
  11.5 1.1 pad_maximum_fusion.1.wg_hbm
  12.6 1.2 dynamic-slice_convert_fusion.6
  13.8 0.8 pad_maximum_fusion.6.wh_ref
  14.6 85.7 %front.1 = (bf16[8,128,1024]{2,1,0:T(8,128)(2,1)}, bf16[8,128,1024]{2,1,0:T(8,128)(2,1)}, bf16[1024,256]{1,0:T(8,128)(2,1)}, bf16[1024,576]{1,0:T(8,128)(2,1)}, ...) custom-call(s32[1,8]{1,0:T(1,128)} %doc_ref.1, ...), custom_call_target="tpu_custom_call" | custom-call | tf_op jit(solution)/shard_map/front/pallas_call | solution.py:591
  100.3 122.9 %feed_forward.1 = (bf16[4,256,1024]{2,1,0:T(8,128)(2,1)}, bf16[8,128,1024]{2,1,0:T(8,128)(2,1)}, f32[128,1024]{1,0:T(8,128)}, f32[128,1024]{1,0:T(8,128)}, bf16[...) custom-call(bf16[4,256,128]{2,1,0:T(8,128)(2,1)} %get-tuple-element., ...), custom_call_target="tpu_custom_call" | custom-call | tf_op jit(solution)/shard_map/feed_forward/pallas_call | solution.py:853
  223.3 1.6 convert_reduce_fusion.1
  225.1 0.9 dynamic-slice_bitcast_fusion.3
  226.0 1.9 collective-permute-start.1
  227.9 8.0 %collective-permute-start.2 = (f32[576,64]{0,1:T(8,128)}, f32[576,64]{0,1:T(8,128)}, u32[]{:S(2)}, u32[]{:S(2)}) collective-permute-start(f32[576,64]{0,1:T(8,128)} %get-tuple-element.114), channel_id=1, source_target_pairs={{0,2},{1,18},{2,0},{3,16},{4,6},{5,22},{6,4},{7,20},{8,10},{9,26},... | collective-permute-start | bytes 442376 | tf_op jit(solution)/shard_map/ppermute | solution.py:1088
  236.3 2.5 multiply_divide_fusion
  240.4 10.0 %attend_back.1 = (f32[1024,128]{1,0:T(8,128)S(1)}, bf16[2,1024,128]{2,1,0:T(8,128)(2,1)S(1)}) custom-call(s32[1]{0:T(128)} %bitcast.9.m_ref, bf16[1024,128]{1,0:T(8,128)(2,1)S(1)} %copy-done.4, bf16[2,1024,128]{2,1,0:T(8,128)(2,1)S(1)} %copy-done.3, s32[1024,1]{1,0:T(8,128)S(1)} %copy.94.begin_ref, bf16[1024,128]{1,0:T(8,128)(2,1)S(1)} %get-tuple-element.108.g_ref, ...), custom_call_target="tpu_custom_call" | custom-call | flops 8589934592 | bytes 8388608 | tf_op jit(solution)/shard_map/attend_back/pallas_call | solution.py:309
  250.5 0.8 copy-done.2
  251.3 9.1 %across_6.1 = bf16[2,1024,128]{2,1,0:T(8,128)(2,1)} custom-call(bf16[2,1024,128]{2,1,0:T(8,128)(2,1)} %copy-done.2), custom_call_target="tpu_custom_call" | custom-call | tf_op jit(solution)/shard_map/across_6/pallas_call | solution.py:137
  260.3 1.2 convert_reduce_fusion.4
  262.9 0.8 copy.97
  264.1 1.0 multiply_add_fusion.1
  267.8 2.3 convolution_convert_fusion.1
  271.5 1.3 pad_maximum_fusion.5
  272.8 6.5 %across_12.1 = bf16[4,512,128]{2,1,0:T(8,128)(2,1)} custom-call(bf16[4,512,128]{2,1,0:T(8,128)(2,1)} %bitcast.143), custom_call_target="tpu_custom_call" | custom-call | tf_op jit(solution)/shard_map/across_12/pallas_call | solution.py:137
  279.3 1.8 convert_reduce_fusion.3
  281.1 6.9 %collective-permute-start = (f32[512,128]{1,0:T(8,128)}, f32[512,128]{1,0:T(8,128)S(1)}, u32[]{:S(2)}, u32[]{:S(2)}) collective-permute-start(f32[512,128]{1,0:T(8,128)} %convert_reduce_fusion.3), channel_id=1, source_target_pairs={{0,0},{1,1},{2,4},{3,5},{4,2},{5,3},{6,6},{7,7},{8,8},{9,9},{10,12... | collective-permute-start | bytes 786440 | tf_op jit(solution)/shard_map/ppermute | solution.py:1121
  288.0 3.6 copy.105
  291.8 2.3 reshape_reshape.3
  294.1 1.0 constant_dynamic-slice_fusion
  295.0 2.4 convolution_convert_fusion.2
  297.8 1.0 copy.107
  298.8 8.7 %across_11.1 = bf16[4,512,64]{2,1,0:T(8,128)(2,1)} custom-call(bf16[4,512,64]{2,1,0:T(8,128)(2,1)} %bitcast.142), custom_call_target="tpu_custom_call" | custom-call | tf_op jit(solution)/shard_map/across_11/pallas_call | solution.py:137
  307.5 1.2 convert_reduce_fusion.2
  309.5 2.1 convolution_convert_fusion
  311.6 29.8 %scatter8_7.1 = f32[128,1024]{1,0:T(8,128)} custom-call(bf16[8,128,1024]{2,1,0:T(8,128)(2,1)} %bitcast.127), custom_call_target="tpu_custom_call" | custom-call | tf_op jit(solution)/shard_map/scatter8_7/pallas_call | solution.py:189
  341.4 1.2 fusion.8
  343.3 7.9 %gather8_13.1 = f32[8,17,128]{2,1,0:T(8,128)} custom-call(f32[17,128]{1,0:T(8,128)} %bitcast.150), custom_call_target="tpu_custom_call" | custom-call | tf_op jit(solution)/shard_map/gather8_13/pallas_call | solution.py:93
  351.2 1.5 reduce_sum.188.x_ref
  352.8 3.9 across_14.1
  356.7 0.8 reduce_sum.189
  358.1 2.1 convert_reduce_fusion
  360.3 1.1 slice_bitcast_fusion
  361.4 29.3 %scatter8_5.1 = f32[128,1024]{1,0:T(8,128)} custom-call(bf16[8,128,1024]{2,1,0:T(8,128)(2,1)} %bitcast.136), custom_call_target="tpu_custom_call" | custom-call | tf_op jit(solution)/shard_map/scatter8_5/pallas_call | solution.py:189
  390.7 1.0 fusion.4
  391.7 0.9 add_bitcast_fusion
  393.2 1.2 pad_maximum_fusion.3
  395.1 1.5 copy.109
  396.5 2.7 reshape.262
  (114 shorter events, 15.2 us)
Async XLA Ops:
  0.6 12.0 %copy-start = (f32[512,1024]{1,0:T(8,128)S(1)}, f32[512,1024]{1,0:T(8,128)}, u32[]{:S(2)}) copy-start(f32[512,1024]{1,0:T(8,128)} %param.20) | copy-start | bytes 6291460
  0.7 3.0 copy-start.20
  0.7 3.6 copy-start.21
  223.3 12.6 %copy-start.22 = (s32[1,8]{1,0:T(1,128)S(1)}, s32[1,8]{1,0:T(1,128)}, u32[]{:S(2)}) copy-start(s32[1,8]{1,0:T(1,128)} %doc_ref.1) | copy-start | bytes 100
  223.3 12.8 %copy-start.7 = (f32[1024,256]{1,0:T(8,128)S(1)}, f32[1024,256]{1,0:T(8,128)}, u32[]{:S(2)}) copy-start(f32[1024,256]{1,0:T(8,128)} %get-tuple-element.57) | copy-start | bytes 3145732
  225.1 11.2 %copy-start.23 = (f32[1024,128]{1,0:T(8,128)S(1)}, f32[1024,128]{1,0:T(8,128)}, u32[]{:S(2)}) copy-start(f32[1024,128]{1,0:T(8,128)} %get-tuple-element.53) | copy-start | bytes 1572868
  226.0 167.2 %collective-permute-start.1 = (f32[576,64]{0,1:T(8,128)}, f32[576,64]{0,1:T(8,128)}, u32[]{:S(2)}, u32[]{:S(2)}) collective-permute-start(f32[576,64]{0,1:T(8,128)} %get-tuple-element.111), channel_id=1, source_target_pairs={{0,0},{1,16},{2,2},{3,18},{4,4},{5,20},{6,6},{7,22},{8,8},{9,24},{... | collective-permute-start | bytes 442376 | tf_op jit(solution)/shard_map/ppermute | solution.py:1088
  227.9 165.2 %collective-permute-start.2 = (f32[576,64]{0,1:T(8,128)}, f32[576,64]{0,1:T(8,128)}, u32[]{:S(2)}, u32[]{:S(2)}) collective-permute-start(f32[576,64]{0,1:T(8,128)} %get-tuple-element.114), channel_id=1, source_target_pairs={{0,2},{1,18},{2,0},{3,16},{4,6},{5,22},{6,4},{7,20},{8,10},{9,26},... | collective-permute-start | bytes 442376 | tf_op jit(solution)/shard_map/ppermute | solution.py:1088
  235.9 157.3 %collective-permute-start.3 = (f32[576,64]{0,1:T(8,128)}, f32[576,64]{0,1:T(8,128)}, u32[]{:S(2)}, u32[]{:S(2)}) collective-permute-start(f32[576,64]{0,1:T(8,128)} %get-tuple-element.113), channel_id=1, source_target_pairs={{0,8},{1,24},{2,10},{3,26},{4,12},{5,28},{6,14},{7,30},{8,0},{9,16... | collective-permute-start | bytes 442376 | tf_op jit(solution)/shard_map/ppermute | solution.py:1088
  235.9 157.3 %collective-permute-start.4 = (f32[576,64]{0,1:T(8,128)}, f32[576,64]{0,1:T(8,128)}, u32[]{:S(2)}, u32[]{:S(2)}) collective-permute-start(f32[576,64]{0,1:T(8,128)} %get-tuple-element.112), channel_id=1, source_target_pairs={{0,10},{1,26},{2,8},{3,24},{4,14},{5,30},{6,12},{7,28},{8,2},{9,18... | collective-permute-start | bytes 442376 | tf_op jit(solution)/shard_map/ppermute | solution.py:1088
  238.8 1.6 copy-start.3
  238.8 1.6 copy-start.4
  250.5 0.8 copy-start.2
  261.5 1.0 copy-start.11
  261.6 1.4 copy-start.10
  264.0 1.4 copy-start.12
  265.3 1.2 copy-start.8
  267.8 2.4 copy-start.15
  281.1 118.2 %collective-permute-start = (f32[512,128]{1,0:T(8,128)}, f32[512,128]{1,0:T(8,128)S(1)}, u32[]{:S(2)}, u32[]{:S(2)}) collective-permute-start(f32[512,128]{1,0:T(8,128)} %convert_reduce_fusion.3), channel_id=1, source_target_pairs={{0,0},{1,1},{2,4},{3,5},{4,2},{5,3},{6,6},{7,7},{8,8},{9,9},{10,12... | collective-permute-start | bytes 786440 | tf_op jit(solution)/shard_map/ppermute | solution.py:1121
  288.0 3.6 copy-start.6
  297.4 12.1 %copy-start.16 = (bf16[1024,64]{0,1:T(8,128)(2,1)S(1)}, bf16[1024,64]{0,1:T(8,128)(2,1)}, u32[]{:S(2)}) copy-start(bf16[1024,64]{0,1:T(8,128)(2,1)} %copy-done.15) | copy-start | bytes 393220
  297.4 12.1 %copy-start.17 = (bf16[1024,256]{1,0:T(8,128)(2,1)S(1)}, bf16[1024,256]{1,0:T(8,128)(2,1)}, u32[]{:S(2)}) copy-start(bf16[1024,256]{1,0:T(8,128)(2,1)} %get-tuple-element.59) | copy-start | bytes 1572868
  311.6 29.9 %copy-start.18 = (f32[1024]{0:T(1024)S(1)}, f32[1024]{0:T(1024)}, u32[]{:S(2)}) copy-start(f32[1024]{0:T(1024)} %param.16) | copy-start | bytes 12292
  311.6 31.1 %copy-start.19 = (f32[1,1024]{1,0:T(1,128)S(1)}, f32[1,1024]{1,0:T(1,128)}, u32[]{:S(2)}) copy-start(f32[1,1024]{1,0:T(1,128)} %get-tuple-element.60) | copy-start | bytes 12292
  360.2 30.4 %copy-start.5 = (f32[128,1024]{1,0:T(8,128)S(1)}, f32[128,1024]{1,0:T(8,128)}, u32[]{:S(2)}) copy-start(f32[128,1024]{1,0:T(8,128)} %scatter8_7.1) | copy-start | bytes 1572868
  361.3 29.3 %copy-start.14 = (f32[128,1024]{1,0:T(8,128)S(1)}, f32[128,1024]{1,0:T(8,128)}, u32[]{:S(2)}) copy-start(f32[128,1024]{1,0:T(8,128)} %get-tuple-element.48) | copy-start | bytes 1572868
  361.3 30.3 %copy-start.13 = (f32[128,1024]{1,0:T(8,128)S(1)}, f32[128,1024]{1,0:T(8,128)}, u32[]{:S(2)}) copy-start(f32[128,1024]{1,0:T(8,128)} %get-tuple-element.46) | copy-start | bytes 1572868
  390.7 1.0 copy-start.9
  395.1 6.7 %copy-start.1 = (f32[512,1024]{1,0:T(8,128)S(1)}, f32[512,1024]{1,0:T(8,128)}, u32[]{:S(2)}) copy-start(f32[512,1024]{1,0:T(8,128)} %param.20) | copy-start | bytes 6291460
where the time goes:
time: 408 us; the launch traced here: 402 us
  Pallas kernels  314 us (77%)
  local copies, waits for them, and re-layouts  33.3 us (8%)
  other arithmetic  27 us (7%)
  starting transfers between devices  16.7 us (4%)
  matrix products  9.28 us (2%)
    pallas_call x1, Pallas kernels, feed_forward(): pl.pallas_call(ffn_kernel, out_shape=(shape((4, BLOCK, WIDTH), bf16), sha...  123 us
    pallas_call x1, Pallas kernels, front(): pl.pallas_call(front_kernel, out_shape=(shape((8, ROWS, WIDTH), bf16), sh...  85.7 us
    pallas_call x2, Pallas kernels, scatter8(): pl.pallas_call(scatter8_kernel, out_shape=jax.ShapeDtypeStruct(shp, f32),...  59.1 us
    pallas_call x4, Pallas kernels, across(): pl.pallas_call(functools.partial(across_kernel, both, same), out_shape=ja...  28.2 us
    pallas_call x1, Pallas kernels, attend_back(): pl.pallas_call(functools.partial(attend_back_kernel, span), out_shape=(ja...  10 us
    ppermute x4, starting transfers between devices, local(): rounds.append(lax.ppermute(piece, ('ctx', 'fsdp'), perm))  9.89 us
  transfers between devices with their start and end apart: 5, of which 0 were waited for; matrix products, arithmetic and copies ran while one was open for 12% of the time, Pallas kernels for 26%

commit v1 on v0

--- a/solution.py
+++ b/solution.py
@@ -344,7 +344,7 @@
 
 
 def front_kernel(
-    doc_ref, x_ref, c_hbm, wh_ref, wg_hbm, wu_hbm, wd_hbm, wo_hbm, again_ref, qgain_ref, kgain_ref,
+    doc_ref, x_ref, c_ref, wh_ref, wg_hbm, wu_hbm, wd_hbm, wo_hbm, again_ref, qgain_ref, kgain_ref,
     x_all, c_all, w_heads, w_gate, w_up, w_down, w_out, q_rows, kv_all, att, summed, totals,
     stacked, normed, cosine, sine,
     s_x, r_x, s_c, r_c, s_h, r_h, s_w, r_w, s_v, r_v, s_o, r_o, s_k, r_k, l_s,
@@ -362,19 +362,8 @@
     me = slot(z, core)
     owner = f == z // 2
 
-    stay = [
-        pltpu.make_async_copy(c_hbm, c_all.at[me], l_s.at[0]),
-        pltpu.make_async_copy(wg_hbm, w_gate.at[pl.ds(f * half_width, half_width)], l_s.at[1]),
-        pltpu.make_async_copy(wu_hbm, w_up.at[pl.ds(f * half_width, half_width)], l_s.at[2]),
-        pltpu.make_async_copy(wo_hbm, w_out.at[pl.ds(f * half_width, half_width)], l_s.at[3]),
-    ]
-    for cp in stay:
-        cp.start()
-    stay_down = pltpu.make_async_copy(wd_hbm, w_down, l_s.at[4])
-
-    @pl.when(owner)
-    def _():
-        stay_down.start()
+    stay = pltpu.make_async_copy(c_ref, c_all.at[me], l_s.at[0])
+    stay.start()
 
     enter([sib, pair] + zpeers + mpeers)
 
@@ -390,7 +379,7 @@
         return gather(x_ref, x_all, s_x, r_x, k)
 
     def c_copy(k):
-        return gather(c_hbm, c_all, s_c, r_c, k)
+        return gather(c_ref, c_all, s_c, r_c, k)
 
     for k in (1, 0, 2, 3):
         x_copy(k).start()
@@ -404,10 +393,9 @@
 
     def w_copy(k, stage):
         src, dst = ((wg_hbm, w_gate), (wu_hbm, w_up), (wd_hbm, w_down), (wo_hbm, w_out))[k]
-        base = 0 if k == 2 else (f if stage == 0 else 1 - f) * half_width
         size = (quarter, quarter, cols // 2, eighth)[k]
         part = hm * 2 + core if k == 3 else hm
-        place = dst.at[pl.ds(pl.multiple_of(base + part * size, 8), size)]
+        place = dst.at[pl.ds(pl.multiple_of(part * size, 8), size)]
         if stage == 0:
             here = src.at[pl.ds(pl.multiple_of(part * size, 8), size)]
             return rcopy(here, place, s_w.at[k], r_w.at[k], pair)
@@ -415,8 +403,7 @@
 
     def out_copy(k):
         part = (hm if k == 0 else 1 - hm) * 2 + core
-        base = (1 - f) * half_width
-        place = w_out.at[pl.ds(pl.multiple_of(base + part * eighth, 8), eighth)]
+        place = w_out.at[pl.ds(pl.multiple_of(part * eighth, 8), eighth)]
         return rcopy(place, place, s_o.at[k], r_o.at[k], sib)
 
     for k in (0, 1, 3):
@@ -540,10 +527,9 @@
 
     def w_got(k):
         dst = (w_gate, w_up, w_down, w_out)[k]
-        base = 0 if k == 2 else (1 - f) * half_width
         size = (quarter, quarter, cols // 2, eighth)[k]
         part = (1 - hm) * 2 + core if k == 3 else 1 - hm
-        place = dst.at[pl.ds(pl.multiple_of(base + part * size, 8), size)]
+        place = dst.at[pl.ds(pl.multiple_of(part * size, 8), size)]
         return rcopy(place, place, s_v.at[k], r_v.at[k], beside)
 
     w_got(3).wait_recv()
@@ -558,15 +544,13 @@
 
     @pl.when(owner)
     def _():
-        stay_down.wait()
         w_copy(2, 0).wait_send()
 
     for k in range(3, 7):
         c_copy(k).wait_recv()
     for k in range(2):
         out_copy(k).wait_recv()
-    for cp in stay:
-        cp.wait()
+    stay.wait()
     heads_copy.wait_send()
     for k in range(7):
         x_copy(k).wait_send()
@@ -594,10 +578,10 @@
             shape((8, ROWS, WIDTH), bf16),
             shape((8, ROWS, WIDTH), bf16),
             shape((WIDTH, 256), bf16),
-            shape((WIDTH, cols), bf16),
-            shape((WIDTH, cols), bf16),
+            shape((WIDTH // 2, cols), bf16),
+            shape((WIDTH // 2, cols), bf16),
             shape((cols, WIDTH), bf16),
-            shape((WIDTH, WIDTH), bf16),
+            shape((WIDTH // 2, WIDTH), bf16),
             shape((tokens, 128), bf16),
             shape((M, tokens, 128), bf16),
             shape((4, BLOCK, 128), bf16),
@@ -609,7 +593,7 @@
             shape((tokens, 128), f32),
         ),
         in_specs=[pl.BlockSpec(memory_space=pltpu.SMEM)]
-        + vspecs(1) + any_specs(1) + vspecs(1) + any_specs(4) + vspecs(3),
+        + vspecs(3) + any_specs(4) + vspecs(3),
         out_specs=tuple(vspecs(1) + any_specs(1) + vspecs(1) + any_specs(4) + vspecs(9)),
         scratch_shapes=[
             sem((7,)), sem((7,)), sem((7,)), sem((7,)), sem((1,)), sem((1,)),
@@ -624,7 +608,8 @@
 
 
 def ffn_kernel(
-    att_ref, x_hbm, c_hbm, own_c_ref, wo_hbm, wg_hbm, wu_hbm, wd_hbm, gain_ref,
+    att_ref, x_hbm, c_hbm, own_c_ref, wo_own, wg_own, wu_own, wd_own, wo_got, wg_got, wu_got, wd_got,
+    gain_ref,
     att_all, branch_ref, gmid_ref, mid_ref, dpart_ref, gpart_ref, glu_rx, down_rx,
     x_v, c_v, wo_v, wg_v, wu_v, wd_v, normed, hid, gg, gu, mid_b, p_out, p_sib, p_sum, p_rx,
     glu_tx, down_tx, br_own,
@@ -643,13 +628,36 @@
     others = [(group + s) % T for s in range(1, T)]
     tpeers = [dev(z, o // 2, core, o % 2) for o in others]
 
-    loads = []
-    for k, (a, b) in enumerate(
-        ((wo_hbm, wo_v), (x_hbm, x_v), (wg_hbm, wg_v), (wu_hbm, wu_v), (c_hbm, c_v), (wd_hbm, wd_v))
-    ):
-        cp = pltpu.make_async_copy(a, b, ld.at[k])
+    mine = pl.ds(pl.multiple_of(f * half_width, half_width), half_width)
+    yours = pl.ds(pl.multiple_of((1 - f) * half_width, half_width), half_width)
+    loads = [
+        pltpu.make_async_copy(a, b, ld.at[k])
+        for k, (a, b) in enumerate(
+            (
+                (wo_own, wo_v.at[mine]),
+                (wo_got, wo_v.at[yours]),
+                (x_hbm, x_v),
+                (wg_own, wg_v.at[mine]),
+                (wg_got, wg_v.at[yours]),
+                (wu_own, wu_v.at[mine]),
+                (wu_got, wu_v.at[yours]),
+                (c_hbm, c_v),
+            )
+        )
+    ]
+    for cp in loads:
         cp.start()
-        loads.append(cp)
+    owner = f == z // 2
+
+    @pl.when(owner)
+    def _():
+        pltpu.make_async_copy(wd_own, wd_v, ld.at[8]).start()
+
+    @pl.when(jnp.logical_not(owner))
+    def _():
+        pltpu.make_async_copy(wd_got, wd_v, ld.at[8]).start()
+
+    loads.append(pltpu.make_async_copy(wd_own, wd_v, ld.at[8]))
     enter([sib] + zpeers + tpeers)
 
     def lanes(j):
@@ -843,7 +851,7 @@
             x_copy(which, s).wait_send()
 
 
-def feed_forward(att, x_all, c_all, own_c, w_out, w_gate, w_up, w_down, gain, cid):
+def feed_forward(att, x_all, c_all, own_c, own_weights, got_weights, gain, cid):
     n = lax.axis_size("ctx")
     T, seg, each = n // 4, FF // n, WIDTH // n
     cols = FF // 8
@@ -862,7 +870,7 @@
             shape((T, 2, seg, half_width), bf16),
             shape((T, cols, 4 * each), bf16),
         ),
-        in_specs=vspecs(1) + any_specs(2) + vspecs(1) + any_specs(4) + vspecs(1),
+        in_specs=vspecs(1) + any_specs(2) + vspecs(1) + any_specs(8) + vspecs(1),
         out_specs=tuple(vspecs(8)),
         scratch_shapes=[
             VS((4, BLOCK, WIDTH), bf16),
@@ -883,7 +891,7 @@
             VS((T, 2, seg, half_width), bf16),
             VS((T, cols, 4 * each), bf16),
             VS((ROWS, WIDTH), bf16),
-            sem((6,)),
+            sem((9,)),
             sem((3, 4)),
             sem((3, 4)),
             sem((4, 4)),
@@ -900,7 +908,412 @@
             collective_id=cid, has_side_effects=True, vmem_limit_bytes=60 * 2**20
         ),
         name="feed_forward",
-    )(att, x_all, c_all, own_c, w_out, w_gate, w_up, w_down, gain)
+    )(att, x_all, c_all, own_c, *own_weights, *got_weights, gain)
+
+
+def back_kernel(
+    doc_ref, branch_ref, att_ref, wo_own, wo_got, q_rows, kv_all, summed, totals, stacked, cosine, sine,
+    normed, w_heads, dpart, mid_ref, gmid_ref, x_ref, again_ref, qgain_ref, kgain_ref, fpart_ref,
+    out_ref, igrad_ref, gains_ref, heads_ref, attn_ref,
+    wo_v, g_v, delta_v, dq_v, dkv_acc, dkv_tx, dkv_rx, gs_v,
+    d_sib, d_sum, d_rx, p_part, p_sib, p_sum, p_rx, h_tx, h_rx, a_tx, a_rx, gn_tx, gn_rx, gt_tx, gt_rx,
+    ld, s_d, r_d, s_p, r_p, s_k, r_k, s_h, r_h, l_h, s_a, r_a, l_a, s_g, r_g, s_t, r_t,
+):
+    z, m, core, f = who()
+    M = lax.axis_size("ctx") // 8
+    T = 2 * M
+    span = lax.axis_size("ctx") // 4 * ROWS
+    each = WIDTH // lax.axis_size("ctx")
+    half_width = WIDTH // 2
+    sib = dev(z, m, 1 - core, f)
+    zs = [(z + s) % 4 for s in (1, 2, 3)]
+    zpeers = [dev(zz, m, core, f) for zz in zs]
+    cross = [dev(zz, m, 1 - core, f) for zz in zs]
+    mpeers = [dev(z, (m + s) % M, core, f) for s in range(1, M)]
+    group = m * 2 + f
+    others = [(group + s) % T for s in range(1, T)]
+    tpeers = [dev(z, o // 2, core, o % 2) for o in others]
+    owner = f == z // 2
+    head = slot(z, core)
+    me = head
+
+    pieces = [(group + s) % T for s in range(T)]
+    rest_to = [core * M + p // 2 for p in pieces]
+    piece_to = [dev(z, rr // 2, rr % 2, p % 2) for rr, p in zip(rest_to, pieces)]
+    to_self = [(rr == m * 2 + core) & (p % 2 == f) for rr, p in zip(rest_to, pieces)]
+    rest = m * 2 + core
+    core_from = rest // M
+    sources = [(group + s) % T for s in range(T)]
+    piece_from = [dev(z, o // 2, core_from, o % 2) for o in sources]
+    from_self = [(core_from == core) & (o == group) for o in sources]
+
+    cp_own = pltpu.make_async_copy(
+        wo_own.at[pl.ds(pl.multiple_of(head % 4 * 128, 128), 128)], wo_v, ld.at[0]
+    )
+    cp_got = pltpu.make_async_copy(
+        wo_got.at[pl.ds(pl.multiple_of(head % 4 * 128, 128), 128)], wo_v, ld.at[0]
+    )
+
+    @pl.when(owner)
+    def _():
+        cp_own.start()
+
+    @pl.when(jnp.logical_not(owner))
+    def _():
+        cp_got.start()
+
+    bar = pltpu.get_barrier_semaphore()
+    fixed = [sib] + zpeers + cross + tpeers
+    for p in fixed:
+        pl.semaphore_signal(bar, inc=1, device_id=p, device_id_type=MESH)
+    for s in range(T):
+
+        @pl.when(jnp.logical_not(from_self[s]))
+        def _(s=s):
+            pl.semaphore_signal(bar, inc=1, device_id=piece_from[s], device_id_type=MESH)
+
+    pl.semaphore_wait(bar, len(fixed) + T - jnp.where(core_from == core, 1, 0))
+
+    def sib_copy(part, buf, ss, rs, i):
+        b = (z + 1 + i) % 4
+        return rcopy(part.at[b, 1 - core], buf.at[i], ss.at[i], rs.at[i], sib)
+
+    def z_copy(sums, rx, ss, rs, i):
+        return rcopy(sums.at[i], rx.at[i], ss.at[4 + i], rs.at[4 + i], zpeers[i])
+
+    def pass_on(part, buf, sums, rx, ss, rs, i):
+        sib_copy(part, buf, ss, rs, i).wait_recv()
+        b = (z + 1 + i) % 4
+        sums[i] = (part[b, core].astype(f32) + buf[i].astype(f32)).astype(bf16)
+        z_copy(sums, rx, ss, rs, i).start()
+
+    def total_of(part, buf, rx, sums, ss, rs):
+        sib_copy(part, buf, ss, rs, 3).wait_recv()
+        total = part[z, core].astype(f32) + buf[3].astype(f32)
+        for i in range(3):
+            z_copy(sums, rx, ss, rs, i).wait_recv()
+            total = total + rx[i].astype(f32)
+        return total
+
+    D = (dpart, d_sib, d_sum, d_rx, s_d, r_d)
+    for i in range(4):
+        sib_copy(dpart, d_sib, s_d, r_d, i).start()
+
+    @pl.when(owner)
+    def _():
+        cp_own.wait()
+
+    @pl.when(jnp.logical_not(owner))
+    def _():
+        cp_got.wait()
+
+    def block_rows(b):
+        return pl.ds(pl.multiple_of(b * BLOCK, BLOCK), BLOCK)
+
+    def mixed(b, _):
+        rows = block_rows(b)
+        br = jnp.concatenate([branch_ref[2 * b], branch_ref[2 * b + 1]], axis=0)
+        gm = back_product(br, wo_v[...])
+        inv = 1.0 / totals[rows, :]
+        g_v[rows, :] = (gm * inv).astype(bf16)
+        w = gm * summed[rows, :] * (inv * inv)
+        low = lax.broadcasted_iota(jnp.int32, w.shape, 1) < 64
+        a = jnp.sum(jnp.where(low, w, 0.0), axis=1, keepdims=True)
+        c = jnp.sum(jnp.where(low, 0.0, w), axis=1, keepdims=True)
+        delta_v[rows, :] = jnp.where(low, a, c)
+        return 0
+
+    lax.fori_loop(0, 4, mixed, 0)
+    for i in range(3):
+        pass_on(*D[:4], s_d, r_d, i)
+
+    dq_v[...] = jnp.zeros_like(dq_v)
+
+    def kv_copy(s):
+        return rcopy(dkv_tx.at[s], dkv_rx.at[s], s_k.at[s], r_k.at[s], mpeers[s])
+
+    def attend(s, _):
+        mm = (m + 1 + s) % M
+        dkv_acc[...] = jnp.zeros_like(dkv_acc)
+        for zz in range(4):
+            rows = slice(zz * BLOCK, (zz + 1) * BLOCK)
+            keys = (zz + 1) * BLOCK
+            token = zz * span + m * BLOCK + lax.broadcasted_iota(jnp.int32, (BLOCK, 1), 0)
+            begin = begin_of(token, doc_ref)
+            for h in range(2):
+                lanes = slice(h * 64, h * 64 + 64)
+                q = q_rows[rows, lanes]
+                g = g_v[rows, lanes]
+                k = kv_all[mm, :keys, :64]
+                v = kv_all[mm, :keys, 64:]
+                e = block_weights(q, k, begin, zz, m, mm, span)
+                dp = back_product(g, v)
+                ds = (e * (dp - delta_v[rows, h * 64 : h * 64 + 1])).astype(bf16)
+                dq_v[rows, lanes] += dot(ds, k)
+                dkv_acc[:keys, :64] += lead_sum(ds, q)
+                dkv_acc[:keys, 64:] += lead_sum(e.astype(bf16), g)
+
+        @pl.when(s < M - 1)
+        def _():
+            dkv_tx[s] = dkv_acc[...].astype(bf16)
+
+            for ss in range(M - 1):
+
+                @pl.when(s == ss)
+                def _(ss=ss):
+                    kv_copy(ss).start()
+
+        return 0
+
+    lax.fori_loop(0, M, attend, 0)
+
+    strip = jnp.concatenate(
+        [branch_ref[j, :, pl.ds(pl.multiple_of(z * 256, 128), 256)] for j in range(8)], axis=0
+    )
+    strip = jnp.concatenate(
+        [
+            jnp.where(
+                core == 0,
+                strip[:, 2 * mm * each : (2 * mm + 1) * each],
+                strip[:, (2 * mm + 1) * each : (2 * mm + 2) * each],
+            )
+            for mm in range(M)
+        ],
+        axis=1,
+    )
+    prod = lead_sum(att_ref[...].reshape(8 * ROWS, WIDTH), strip).astype(bf16)
+    for mm in range(M):
+        for ff in range(2):
+            a_tx[mm * 2 + ff] = prod[
+                ff * half_width : (ff + 1) * half_width, mm * each : (mm + 1) * each
+            ]
+
+    def a_copy(s):
+        return rcopy(a_tx.at[others[s]], a_rx.at[group], s_a.at[s], r_a.at[s], tpeers[s])
+
+    for s in range(M - 1):
+        kv_copy(s).wait_recv()
+    for s in range(T - 1):
+        a_copy(s).start()
+    a_own = pltpu.make_async_copy(a_tx.at[group], a_rx.at[group], l_a.at[0])
+    a_own.start()
+
+    qgain = qgain_ref[...]
+    kgain = kgain_ref[...]
+
+    def head_mean(v):
+        low = lax.broadcasted_iota(jnp.int32, v.shape, 1) < 64
+        a = jnp.sum(jnp.where(low, v, 0.0), axis=1, keepdims=True)
+        c = jnp.sum(jnp.where(low, 0.0, v), axis=1, keepdims=True)
+        return jnp.where(low, a, c) * (1.0 / 64)
+
+    def heads_back(i, carry):
+        qg, kg = carry
+        b = (z + 1 + i) % 4
+        rows = block_rows(b)
+        co = cosine[rows, :]
+        si = sine[rows, :]
+
+        def through(v, dy, gain):
+            dy = dy * co - turn(dy) * si
+            r = head_scale(v)
+            gdy = gain * dy
+            dv = r * gdy - v * (r * r * r) * head_mean(v * gdy)
+            return dv, jnp.sum(dy * v * r, axis=0, keepdims=True)
+
+        st = stacked[rows, :]
+        dq, qpart = through(st[:, :128], dq_v[rows, :] * HEAD_SIZE ** (-0.5), qgain)
+        dkv = dkv_acc[rows, :]
+        for s in range(M - 1):
+            dkv = dkv + dkv_rx[s, rows, :].astype(f32)
+        dk, kpart = through(st[:, 128:], dkv, kgain)
+        low = lax.broadcasted_iota(jnp.int32, dkv.shape, 1) < 64
+        gs = jnp.concatenate([dq, jnp.where(low, dk, dkv)], axis=1).astype(bf16)
+        gs_v[rows, :] = gs
+        pb = back_product(gs, w_heads[...]).astype(bf16)
+        p_part[b, 0] = pb[:ROWS]
+        p_part[b, 1] = pb[ROWS:]
+        sib_copy(p_part, p_sib, s_p, r_p, i).start()
+        return qg + qpart, kg + kpart
+
+    zero = jnp.zeros((1, 128), f32)
+    qg, kg = lax.fori_loop(0, 4, heads_back, (zero, zero))
+    for i in range(3):
+        pass_on(p_part, p_sib, p_sum, p_rx, s_p, r_p, i)
+
+    prod = lead_sum(normed[...], gs_v[...]).astype(bf16)
+    qw, kw = 128 // M, 64 // M
+    for i in range(M):
+        for ff in range(2):
+            rows = slice(ff * half_width, (ff + 1) * half_width)
+            h_tx[i * 2 + ff] = jnp.concatenate(
+                [
+                    prod[rows, i * qw : (i + 1) * qw],
+                    prod[rows, 128 + i * kw : 128 + (i + 1) * kw],
+                    prod[rows, 192 + i * kw : 192 + (i + 1) * kw],
+                ],
+                axis=1,
+            )
+
+    def h_copy(s):
+        return rcopy(
+            h_tx.at[pieces[s]], h_rx.at[group], s_h.at[s], r_h.at[group], piece_to[s]
+        )
+
+    def h_own(s):
+        return pltpu.make_async_copy(h_tx.at[pieces[s]], h_rx.at[group], l_h.at[0])
+
+    def h_got(s):
+        return rcopy(
+            h_tx.at[pieces[s]], h_rx.at[sources[s]], s_h.at[s], r_h.at[sources[s]], piece_from[s]
+        )
+
+    for s in range(T):
+
+        @pl.when(to_self[s])
+        def _(s=s):
+            h_own(s).start()
+
+        @pl.when(jnp.logical_not(to_self[s]))
+        def _(s=s):
+            h_copy(s).start()
+
+    out_ref[...] = mid_ref[...] + total_of(dpart, d_sib, d_rx, d_sum, s_d, r_d)
+    dy = total_of(p_part, p_sib, p_rx, p_sum, s_p, r_p)
+    x = x_ref[...].astype(f32)
+    r = lax.rsqrt(jnp.mean(x * x, axis=-1, keepdims=True) + epsilon)
+    gdy = again_ref[...] * dy
+    dv = r * gdy - x * (r * r * r) * jnp.mean(x * gdy, axis=-1, keepdims=True)
+    igrad_ref[...] = gmid_ref[...] + dv
+
+    gn_tx[0:1, :] = jnp.sum(dy * x * r, axis=0, keepdims=True)
+    gn_tx[1:2, :] = fpart_ref[...]
+    gn_tx[2:3, :] = jnp.concatenate(
+        [qg, kg, jnp.zeros((1, WIDTH - 256), f32)], axis=1
+    )
+    gpeers = [sib] + zpeers + cross
+
+    def g_copy(k):
+        return rcopy(gn_tx, gn_rx.at[k], s_g.at[k], r_g.at[k], gpeers[k])
+
+    for k in range(7):
+        g_copy(k).start()
+    total = gn_tx[...]
+    for k in range(7):
+        g_copy(k).wait_recv()
+    for k in range(7):
+        total = total + gn_rx[k]
+    gt_tx[...] = total
+
+    def t_copy(s):
+        return rcopy(gt_tx, gt_rx.at[s], s_t.at[s], r_t.at[s], tpeers[s])
+
+    for s in range(T - 1):
+        t_copy(s).start()
+
+    for s in range(T):
+
+        @pl.when(from_self[s])
+        def _(s=s):
+            pltpu.make_async_copy(h_tx.at[0], h_rx.at[group], l_h.at[0]).wait()
+
+        @pl.when(jnp.logical_not(from_self[s]))
+        def _(s=s):
+            h_got(s).wait_recv()
+
+    for s in range(T - 1):
+        a_copy(s).wait_recv()
+    a_own.wait()
+    hsum = h_rx[0].astype(f32)
+    asum = a_rx[0].astype(f32)
+    for k in range(1, T):
+        hsum = hsum + h_rx[k].astype(f32)
+        asum = asum + a_rx[k].astype(f32)
+    heads_ref[...] = hsum
+    attn_ref[...] = asum
+
+    for s in range(T - 1):
+        t_copy(s).wait_recv()
+        total = total + gt_rx[s]
+    gains_ref[...] = total
+
+    for i in range(4):
+        sib_copy(dpart, d_sib, s_d, r_d, i).wait_send()
+        sib_copy(p_part, p_sib, s_p, r_p, i).wait_send()
+    for i in range(3):
+        z_copy(d_sum, d_rx, s_d, r_d, i).wait_send()
+        z_copy(p_sum, p_rx, s_p, r_p, i).wait_send()
+    for s in range(M - 1):
+        kv_copy(s).wait_send()
+    for s in range(T):
+
+        @pl.when(jnp.logical_not(to_self[s]))
+        def _(s=s):
+            h_copy(s).wait_send()
+
+    for s in range(T - 1):
+        a_copy(s).wait_send()
+        t_copy(s).wait_send()
+    for k in range(7):
+        g_copy(k).wait_send()
+
+
+def back(*args, cid):
+    n = lax.axis_size("ctx")
+    M, T, each = n // 8, n // 4, WIDTH // n
+    tokens = 8 * ROWS
+    half_width = WIDTH // 2
+    VS, sem = pltpu.VMEM, pltpu.SemaphoreType.DMA
+    shape = jax.ShapeDtypeStruct
+    part = (ROWS, WIDTH)
+    return pl.pallas_call(
+        back_kernel,
+        out_shape=(
+            shape(part, f32),
+            shape(part, f32),
+            shape((3, WIDTH), f32),
+            shape((half_width, 256 // M), f32),
+            shape((half_width, each), f32),
+        ),
+        in_specs=[pl.BlockSpec(memory_space=pltpu.SMEM)] + vspecs(2) + any_specs(2) + vspecs(17),
+        out_specs=tuple(vspecs(5)),
+        scratch_shapes=[
+            VS((128, WIDTH), bf16),
+            VS((tokens, 128), bf16),
+            VS((tokens, 128), f32),
+            VS((tokens, 128), f32),
+            VS((tokens, 128), f32),
+            VS((M - 1, tokens, 128), bf16),
+            VS((M - 1, tokens, 128), bf16),
+            VS((tokens, 256), bf16),
+            VS((4,) + part, bf16),
+            VS((3,) + part, bf16),
+            VS((3,) + part, bf16),
+            VS((4, 2) + part, bf16),
+            VS((4,) + part, bf16),
+            VS((3,) + part, bf16),
+            VS((3,) + part, bf16),
+            VS((T, half_width, 256 // M), bf16),
+            VS((T, half_width, 256 // M), bf16),
+            VS((T, half_width, each), bf16),
+            VS((T, half_width, each), bf16),
+            VS((3, WIDTH), f32),
+            VS((7, 3, WIDTH), f32),
+            VS((3, WIDTH), f32),
+            VS((T - 1, 3, WIDTH), f32),
+            sem((1,)),
+            sem((7,)), sem((7,)), sem((7,)), sem((7,)),
+            sem((M - 1,)), sem((M - 1,)),
+            sem((T,)), sem((T,)), sem((1,)),
+            sem((T - 1,)), sem((T - 1,)), sem((1,)),
+            sem((7,)), sem((7,)),
+            sem((T - 1,)), sem((T - 1,)),
+        ],
+        compiler_params=pltpu.CompilerParams(
+            collective_id=cid, has_side_effects=True, vmem_limit_bytes=60 * 2**20
+        ),
+        name="back",
+    )(*args)
 
 
 def root_mean_norm(rows, gain):
@@ -988,6 +1401,8 @@
     out_own = attn_proj.astype(bf16)
 
     cotangent = out_cotangent[0]
+    q_gain = jnp.tile(query_gain, 2)[None]
+    k_gain = jnp.concatenate([key_norm_gain, jnp.ones((64,), f32)])[None]
     (
         x_rows, c_rows, w_heads, w_gate, w_up, w_down, w_out, q_rows, kv_all, att_own, summed, totals,
         stacked, normed, cos_table, sin_table,
@@ -1001,66 +1416,45 @@
         down_own,
         out_own,
         attn_gain[None],
-        jnp.tile(query_gain, 2)[None],
-        jnp.concatenate([key_norm_gain, jnp.ones((64,), f32)])[None],
+        q_gain,
+        k_gain,
         1,
     )
-    starts = jnp.cumsum(doc_lengths[0]) - doc_lengths[0]
-    token_index = (
-        jnp.arange(4, dtype=jnp.int32)[:, None] * span
-        + m * BLOCK
-        + jnp.arange(BLOCK, dtype=jnp.int32)[None, :]
-    ).reshape(tokens, 1)
-    after = token_index >= starts[None, :]
-    begins = jnp.max(jnp.where(after, starts[None, :], 0), axis=1, keepdims=True)
-    cosine = cos_table[:, None, :32]
-    sine = sin_table[:, None, 32:64]
-
-    def rotate(q_in, k_in, q_gain, k_gain):
-        q_out = (
-            rotary(root_mean_norm(q_in.reshape(tokens, 2, HEAD_SIZE), q_gain), cosine, sine)
-            * HEAD_SIZE ** (-0.5)
-        )
-        k_out = rotary(root_mean_norm(k_in.reshape(tokens, 1, HEAD_SIZE), k_gain), cosine, sine)
-        return q_out.reshape(tokens, 128), k_out.reshape(tokens, 64)
-
-    _, heads_back = jax.vjp(
-        rotate, stacked[:, :128], stacked[:, 128:192], query_gain, key_norm_gain
-    )
-    m_arr = jnp.full((1,), m, jnp.int32)
     attended, branch, grad_middle, own, down_parts, ffn_gain_part, glu_got, down_got = feed_forward(
         att_own,
         x_rows.reshape(4, BLOCK, WIDTH),
         c_rows.reshape(4, BLOCK, WIDTH),
         cotangent,
-        w_out,
-        w_gate,
-        w_up,
-        w_down,
+        (out_own, gate_own, up_own, down_own),
+        (w_out, w_gate, w_up, w_down),
         ffn_gain[None],
         4,
     )
-    attended = attended.reshape(tokens, WIDTH)
-    branch = branch.reshape(tokens, WIDTH)
-    ffn_gain_part = ffn_gain_part[0]
-    output = own + scatter8(down_parts.reshape(8, ROWS, WIDTH), 5)
-
-    w_out_head = lax.dynamic_slice(w_out, (head * 128, 0), (128, WIDTH))
-    grad_mixed = back_product(branch, w_out_head)
-    grad_summed = (grad_mixed / totals).astype(bf16)
-    weighted = (grad_mixed * summed / (totals * totals)).reshape(tokens, 2, 64)
-    delta = jnp.broadcast_to(
-        jnp.sum(weighted, axis=2, keepdims=True), (tokens, 2, 64)
-    ).reshape(tokens, 128)
-    grad_q, dkv = attend_back(m_arr, q_rows, kv_all, begins, grad_summed, delta, span)
-    dkv = jnp.sum(across(dkv, False, False, 6).astype(f32), axis=0)
-    gq_pre, gk_pre, q_gain_part, k_gain_part = heads_back((grad_q, dkv[:, :64]))
-    grad_stacked = jnp.concatenate([gq_pre, gk_pre, dkv[:, 64:]], axis=1).astype(bf16)
-    part_normed = back_product(grad_stacked, w_heads).reshape(8, ROWS, WIDTH).astype(bf16)
-    grad_normed = scatter8(part_normed, 7)
-    _, attn_back = jax.vjp(root_mean_norm, hidden_in[0].astype(f32), attn_gain)
-    grad_resid, attn_gain_part = attn_back(grad_normed)
-    input_grad = grad_middle + grad_resid
+    output, input_grad, gains, heads_grad, attn_grad = back(
+        doc_lengths,
+        branch,
+        attended,
+        out_own,
+        w_out,
+        q_rows,
+        kv_all,
+        summed,
+        totals,
+        stacked,
+        cos_table,
+        sin_table,
+        normed,
+        w_heads,
+        down_parts,
+        own,
+        grad_middle,
+        hidden_in[0],
+        attn_gain[None],
+        q_gain,
+        k_gain,
+        ffn_gain_part,
+        cid=7,
+    )
 
     glu_grad = jnp.sum(glu_got.astype(f32), axis=0)
     down_sum = jnp.sum(down_got.astype(f32), axis=0)
@@ -1093,46 +1487,18 @@
         rounds.reshape(2, 2, M, segment, each), (0, 2, 1, 3, 4)
     ).reshape(FF // 2, each)
 
-    branch_columns = lax.dynamic_slice(
-        branch.reshape(tokens, 4, M, 2, each), (0, z, 0, core, 0), (tokens, 1, M, 1, each)
-    ).reshape(tokens, M * each)
-    attn_part = lead_sum(attended, branch_columns).astype(bf16)
-    attn_part = jnp.transpose(
-        attn_part.reshape(2, half_width, M, each), (2, 0, 1, 3)
-    ).reshape(T, half_width, each)
-    attn_grad = jnp.sum(across(attn_part, True, False, 11).astype(f32), axis=0)
-
-    heads_part = lead_sum(normed, grad_stacked).astype(bf16)
     qw, kw = 128 // M, 64 // M
-    heads_part = jnp.concatenate(
-        [
-            heads_part[:, :128].reshape(2, half_width, M, qw),
-            heads_part[:, 128:192].reshape(2, half_width, M, kw),
-            heads_part[:, 192:].reshape(2, half_width, M, kw),
-        ],
-        axis=3,
-    )
-    heads_part = jnp.transpose(heads_part, (2, 0, 1, 3)).reshape(T, half_width, 256 // M)
-    heads_grad = jnp.sum(across(heads_part, True, False, 12).astype(f32), axis=0)
-    perm = [
-        (number(zz, mm, cc, ff), number(zz, (cc * M + mm) // 2, (cc * M + mm) % 2, ff))
-        for zz, mm, cc, ff in devices
-    ]
-    heads_grad = lax.ppermute(heads_grad, ("ctx", "fsdp"), perm)
     query_grad = heads_grad[:, :qw]
     key_grad = heads_grad[:, qw : qw + kw]
     value_grad = heads_grad[:, qw + kw :]
 
-    gains = jnp.concatenate([attn_gain_part, ffn_gain_part, q_gain_part, k_gain_part])
-    gains = jnp.sum(gather8(gains.reshape(17, 128), 13), axis=0)
-    gains = jnp.sum(across(gains, True, True, 14), axis=0).reshape(-1)
     return (
         output[None],
         input_grad[None],
-        gains[:WIDTH],
-        gains[2 * WIDTH : 2 * WIDTH + 64],
-        gains[2 * WIDTH + 64 :],
-        gains[WIDTH : 2 * WIDTH],
+        gains[0],
+        gains[2, :64] + gains[2, 64:128],
+        gains[2, 128:192],
+        gains[1],
         query_grad,
         key_grad,
         value_grad,

time: 408 us -> 296 us (0.73)
  the two profiles are of different devices: /device:TPU:13 before, /device:TPU:0 now
where the time goes in v1:
time: 296 us; the launch traced here: 291 us
  Pallas kernels  254 us (86%)
  local copies, waits for them, and re-layouts  21.7 us (7%)
  other arithmetic  11.3 us (4%)
    pallas_call x1, Pallas kernels, feed_forward(): pl.pallas_call(ffn_kernel, out_shape=(shape((4, BLOCK, WIDTH), bf16), sha...  111 us
    pallas_call x1, Pallas kernels, back(): pl.pallas_call(back_kernel, out_shape=(shape(part, f32), shape(part, f32)...  83.7 us
    pallas_call x1, Pallas kernels, front(): pl.pallas_call(front_kernel, out_shape=(shape((8, ROWS, WIDTH), bf16), sh...  59.4 us
    unnamed x20, local copies, waits for them, and re-layouts  6.69 us
  transfers between devices with their start and end apart: 4, of which 0 were waited for; matrix products, arithmetic and copies ran while one was open for 3% of the time, Pallas kernels for 29%

profile of v1, /device:TPU:0, one launch (start us, length us, event | category | flops | bytes accessed | tf_op | source)
XLA Modules:
  0.0 291.1 jit_solution(9501850399926556316)
XLA Ops:
  0.6 0.0 copy-start
  0.7 0.0 copy-start.5
  0.7 0.0 copy-start.6
  0.8 2.9 convert_element_type.6.wo_hbm.wo_own
  3.7 0.0 copy-done.5
  3.7 0.6 broadcast_in_dim_tile.3.qgain_ref
  4.3 0.5 pad_bitcast_fusion.kgain_ref
  4.8 1.8 dynamic-slice_convert_fusion.1
  6.6 1.1 pad_maximum_fusion.wd_hbm.wd_own
  7.7 2.8 dynamic-slice_convert_fusion.3
  10.5 1.1 pad_maximum_fusion.2.wu_hbm.wu_own
  11.6 1.1 pad_maximum_fusion.1.wg_hbm.wg_own
  12.6 0.0 copy-done
  12.7 1.2 dynamic-slice_convert_fusion.6
  13.9 0.8 pad_maximum_fusion.4.wh_ref
  14.7 59.4 %front.1 = (bf16[8,128,1024]{2,1,0:T(8,128)(2,1)}, bf16[8,128,1024]{2,1,0:T(8,128)(2,1)}, bf16[1024,256]{1,0:T(8,128)(2,1)}, bf16[512,576]{1,0:T(8,128)(2,1)}, b...) custom-call(s32[1,8]{1,0:T(1,128)} %doc_ref.3, ...), custom_call_target="tpu_custom_call" | custom-call | tf_op jit(solution)/shard_map/front/pallas_call | solution.py:575
  74.1 111.1 %feed_forward.1 = (bf16[4,256,1024]{2,1,0:T(8,128)(2,1)}, bf16[8,128,1024]{2,1,0:T(8,128)(2,1)}, f32[128,1024]{1,0:T(8,128)}, f32[128,1024]{1,0:T(8,128)}, bf16[...) custom-call(bf16[4,256,128]{2,1,0:T(8,128)(2,1)} %get-tuple-element., ...), custom_call_target="tpu_custom_call" | custom-call | tf_op jit(solution)/shard_map/feed_forward/pallas_call | solution.py:861
  185.2 1.5 convert_reduce_fusion.1
  186.7 0.2 copy.40
  187.0 0.1 dynamic-slice_bitcast_fusion.3
  187.0 0.7 collective-permute-start
  187.7 0.1 collective-permute-start.1
  187.8 1.8 collective-permute-start.2
  189.6 0.1 collective-permute-start.3
  189.7 2.1 convert_reduce_fusion
  191.8 1.1 slice_bitcast_fusion
  192.9 83.7 %back.1 = (f32[128,1024]{1,0:T(8,128)}, f32[128,1024]{1,0:T(8,128)}, f32[3,1024]{1,0:T(4,128)}, f32[512,128]{1,0:T(8,128)}, f32[512,64]{1,0:T(8,128)}) custom-call(s32[1,8]{1,0:T(1,128)} %doc_ref.3, bf16[8,128,1024]{2,1,0:T(8,128)(2,1)} %get-tuple-element.49.branch_ref, bf16[4,256,1024]{2,1,0:T(8,128)(2,1)} %get-tuple-element.50.att_ref, ...), custom_call_target="tpu_custom_call" | custom-call | tf_op jit(solution)/shard_map/back/pallas_call | solution.py:1269
  276.7 1.3 fusion
  278.0 0.7 copy.43
  278.7 0.7 copy.44
  279.4 1.7 copy.42
  281.2 0.0 copy-done.3
  281.2 0.8 copy.45
  281.9 0.0 copy-done.4
  281.9 0.6 fusion.1
  282.5 0.6 slice_bitcast_fusion.2
  283.1 0.0 collective-permute-done
  283.1 0.0 collective-permute-done.1
  283.1 0.0 collective-permute-done.2
  283.1 0.0 collective-permute-done.3
  283.3 0.6 reshape.66
  283.9 0.0 copy-start.2
  283.9 0.0 copy-start.1
  283.9 1.5 copy.41
  285.4 2.7 reshape.67
  288.2 1.9 copy.48
  290.0 0.0 copy-done.2
  290.0 0.8 copy.49
  (9 shorter events, 0.2 us)
Async XLA Ops:
  0.6 12.0 %copy-start = (f32[512,1024]{1,0:T(8,128)S(1)}, f32[512,1024]{1,0:T(8,128)}, u32[]{:S(2)}) copy-start(f32[512,1024]{1,0:T(8,128)} %param.20) | copy-start | bytes 6291460
  0.7 3.0 %copy-start.5 = (f32[64]{0:T(128)S(1)}, f32[64]{0:T(128)}, u32[]{:S(2)}) copy-start(f32[64]{0:T(128)} %param.17) | copy-start | bytes 772
  0.7 3.6 %copy-start.6 = (f32[64]{0:T(128)S(1)}, f32[64]{0:T(128)}, u32[]{:S(2)}) copy-start(f32[64]{0:T(128)} %param.18) | copy-start | bytes 772
  187.0 96.1 %collective-permute-start = (f32[576,64]{0,1:T(8,128)S(1)}, f32[576,64]{0,1:T(8,128)S(1)}, u32[]{:S(2)}, u32[]{:S(2)}) collective-permute-start(f32[576,64]{0,1:T(8,128)S(1)} %get-tuple-element.131), channel_id=1, source_target_pairs={{0,0},{1,16},{2,2},{3,18},{4,4},{5,20},{6,6},{7,22},{8,8},{9,24},{... | collective-permute-start | bytes 442376 | tf_op jit(solution)/shard_map/ppermute | solution.py:1482
  187.7 95.4 %collective-permute-start.1 = (f32[576,64]{0,1:T(8,128)S(1)}, f32[576,64]{0,1:T(8,128)S(1)}, u32[]{:S(2)}, u32[]{:S(2)}) collective-permute-start(f32[576,64]{0,1:T(8,128)S(1)} %get-tuple-element.134), channel_id=1, source_target_pairs={{0,2},{1,18},{2,0},{3,16},{4,6},{5,22},{6,4},{7,20},{8,10},{9,26},... | collective-permute-start | bytes 442376 | tf_op jit(solution)/shard_map/ppermute | solution.py:1482
  187.8 95.3 %collective-permute-start.2 = (f32[576,64]{0,1:T(8,128)S(1)}, f32[576,64]{0,1:T(8,128)S(1)}, u32[]{:S(2)}, u32[]{:S(2)}) collective-permute-start(f32[576,64]{0,1:T(8,128)S(1)} %get-tuple-element.133), channel_id=1, source_target_pairs={{0,8},{1,24},{2,10},{3,26},{4,12},{5,28},{6,14},{7,30},{8,0},{9,16... | collective-permute-start | bytes 442376 | tf_op jit(solution)/shard_map/ppermute | solution.py:1482
  189.6 93.5 %collective-permute-start.3 = (f32[576,64]{0,1:T(8,128)S(1)}, f32[576,64]{0,1:T(8,128)S(1)}, u32[]{:S(2)}, u32[]{:S(2)}) collective-permute-start(f32[576,64]{0,1:T(8,128)S(1)} %get-tuple-element.132), channel_id=1, source_target_pairs={{0,10},{1,26},{2,8},{3,24},{4,14},{5,30},{6,12},{7,28},{8,2},{9,18... | collective-permute-start | bytes 442376 | tf_op jit(solution)/shard_map/ppermute | solution.py:1482
  276.7 4.5 %copy-start.3 = (f32[512,64]{1,0:T(8,128)S(1)}, f32[512,64]{1,0:T(8,128)}, u32[]{:S(2)}) copy-start(f32[512,64]{1,0:T(8,128)} %get-tuple-element.119) | copy-start | bytes 393220
  276.7 5.3 %copy-start.4 = (f32[3,1024]{1,0:T(4,128)S(1)}, f32[3,1024]{1,0:T(4,128)}, u32[]{:S(2)}) copy-start(f32[3,1024]{1,0:T(4,128)} %get-tuple-element.66) | copy-start | bytes 36868
  283.9 6.2 %copy-start.2 = (f32[128,1024]{1,0:T(8,128)S(1)}, f32[128,1024]{1,0:T(8,128)}, u32[]{:S(2)}) copy-start(f32[128,1024]{1,0:T(8,128)} %get-tuple-element.65) | copy-start | bytes 1572868
  283.9 6.9 %copy-start.1 = (f32[512,1024]{1,0:T(8,128)S(1)}, f32[512,1024]{1,0:T(8,128)}, u32[]{:S(2)}) copy-start(f32[512,1024]{1,0:T(8,128)} %param.20) | copy-start | bytes 6291460

commit v2 on v1

--- a/solution.py
+++ b/solution.py
@@ -60,151 +60,152 @@
     return [pl.BlockSpec(memory_space=ANY)] * n
 
 
-def gather8_kernel(x_ref, o_ref, ss, rs, ls):
-    z, m, core, f = who()
-    sib = dev(z, m, 1 - core, f)
-    peers = [dev((z + s) % 4, m, core, f) for s in (1, 2, 3)]
-    me = slot(z, core)
-    own = pltpu.make_async_copy(x_ref, o_ref.at[me], ls)
-    own.start()
-    enter([sib] + peers)
-    first = []
-    for k in (1, 0, 2):
-        cp = rcopy(x_ref, o_ref.at[me], ss.at[k], rs.at[k], peers[k])
-        cp.start()
-        first.append((k, cp))
-    cp0 = rcopy(x_ref, o_ref.at[me], ss.at[3], rs.at[3], sib)
-    cp0.start()
-    fw = []
-    for k, cp in first:
-        sl = slot((z + 3 - k) % 4, core)
-        cp.wait_recv()
-        cp = rcopy(o_ref.at[sl], o_ref.at[sl], ss.at[4 + k], rs.at[4 + k], sib)
-        cp.start()
-        fw.append(cp)
-    for cp in fw + [cp0]:
-        cp.wait_recv()
-    for cp in [cp for _, cp in first] + [cp0] + fw:
-        cp.wait_send()
-    own.wait()
-
-
-def gather8(x, cid):
-    return pl.pallas_call(
-        gather8_kernel,
-        out_shape=jax.ShapeDtypeStruct((8,) + x.shape, x.dtype),
-        in_specs=any_specs(1),
-        out_specs=any_specs(1)[0],
-        scratch_shapes=[
-            pltpu.SemaphoreType.DMA((7,)),
-            pltpu.SemaphoreType.DMA((7,)),
-            pltpu.SemaphoreType.DMA,
-        ],
-        compiler_params=comm_params(cid),
-        name="gather8_%d" % cid,
-    )(x)
-
-
-def across_kernel(both, same, x_ref, o_ref, ss, rs, ls):
-    z, m, core, f = who()
-    M = lax.axis_size("ctx") // 8
-    count = M * 2 if both else M
-    me = m * 2 + f if both else m
-    others = [(me + s) % count for s in range(1, count)]
-    peers = [dev(z, o // 2, core, o % 2) if both else dev(z, o, core, f) for o in others]
-
-    def src(k):
-        return x_ref if same else x_ref.at[k]
-
-    own = pltpu.make_async_copy(src(me), o_ref.at[me], ls)
-    own.start()
-    enter(peers)
-    cps = []
-    for s in range(count - 1):
-        cp = rcopy(src(others[s]), o_ref.at[me], ss.at[s], rs.at[s], peers[s])
-        cp.start()
-        cps.append(cp)
-    for cp in cps:
-        cp.wait_recv()
-    for cp in cps:
-        cp.wait_send()
-    own.wait()
-
-
-def across(x, both, same, cid):
-    shp = x.shape if same else x.shape[1:]
-    count = lax.axis_size("ctx") // (4 if both else 8)
-    return pl.pallas_call(
-        functools.partial(across_kernel, both, same),
-        out_shape=jax.ShapeDtypeStruct((count,) + shp, x.dtype),
-        in_specs=any_specs(1),
-        out_specs=any_specs(1)[0],
-        scratch_shapes=[
-            pltpu.SemaphoreType.DMA((count - 1,)),
-            pltpu.SemaphoreType.DMA((count - 1,)),
-            pltpu.SemaphoreType.DMA,
-        ],
-        compiler_params=comm_params(cid),
-        name="across_%d" % cid,
-    )(x)
-
-
-def scatter8_kernel(x_ref, o_ref, a, b, s_buf, d, ls, s1, r1, s2, r2):
-    z, m, core, f = who()
-    sib = dev(z, m, 1 - core, f)
-    to = [(z + s) % 4 for s in (1, 2, 3, 0)]
-    peers = [dev(zz, m, core, f) for zz in to[:3]]
-    loads = []
-    for k in range(4):
-        cp = pltpu.make_async_copy(x_ref.at[slot(to[k], core)], a.at[k], ls.at[k])
-        cp.start()
-        loads.append(cp)
-    enter([sib] + peers)
-    ones = []
-    for k in range(4):
-        cp = rcopy(x_ref.at[slot(to[k], 1 - core)], b.at[k], s1.at[k], r1.at[k], sib)
-        cp.start()
-        ones.append(cp)
-    twos = []
-    for k in range(3):
-        loads[k].wait()
-        ones[k].wait_recv()
-        s_buf[k] = (a[k].astype(f32) + b[k].astype(f32)).astype(s_buf.dtype)
-        cp = rcopy(s_buf.at[k], d.at[k], s2.at[k], r2.at[k], peers[k])
-        cp.start()
-        twos.append(cp)
-    loads[3].wait()
-    ones[3].wait_recv()
-    total = a[3].astype(f32) + b[3].astype(f32)
-    for k in range(3):
-        twos[k].wait_recv()
-        total = total + d[k].astype(f32)
-    o_ref[...] = total
-    for cp in ones + twos:
-        cp.wait_send()
-
-
-def scatter8(x, cid):
-    shp = x.shape[1:]
-    return pl.pallas_call(
-        scatter8_kernel,
-        out_shape=jax.ShapeDtypeStruct(shp, f32),
-        in_specs=any_specs(1),
-        out_specs=pl.BlockSpec(memory_space=pltpu.VMEM),
-        scratch_shapes=[
-            pltpu.VMEM((4,) + shp, x.dtype),
-            pltpu.VMEM((4,) + shp, x.dtype),
-            pltpu.VMEM((3,) + shp, x.dtype),
-            pltpu.VMEM((3,) + shp, x.dtype),
-            pltpu.SemaphoreType.DMA((4,)),
-            pltpu.SemaphoreType.DMA((4,)),
-            pltpu.SemaphoreType.DMA((4,)),
-            pltpu.SemaphoreType.DMA((3,)),
-            pltpu.SemaphoreType.DMA((3,)),
-        ],
-        compiler_params=comm_params(cid),
-        name="scatter8_%d" % cid,
-    )(x)
+def line_of(z):
+    return z + 1 - 2 * (z % 2), 2 - z // 2, 3 - 3 * (z // 2), 1 - ((z + 1) // 2) % 2
+
+
+def packed(v):
+    rows, cols = v.shape
+    n = 128 // cols
+    size = rows // n
+    return jnp.concatenate([v[g * size : (g + 1) * size] for g in range(n)], axis=1)
+
+
+class Gather:
+    def __init__(self, src, dst, ss, rs):
+        z, m, core, f = who()
+        partner, middle, end, self.at_end = line_of(z)
+        self.src, self.dst, self.ss, self.rs = src, dst, ss, rs
+        self.me = slot(z, core)
+        self.slots = [slot(zz, core) for zz in (partner, middle, end)]
+        self.partner = dev(partner, m, core, f)
+        self.middle = dev(middle, m, core, f)
+        self.sib = dev(z, m, 1 - core, f)
+
+    def copy(self, k):
+        src, dst, ss, rs = self.src, self.dst, self.ss.at[k], self.rs
+        if k == 0:
+            return rcopy(src, dst.at[self.me], ss, rs.at[0], self.partner)
+        if k == 1:
+            return rcopy(src, dst.at[self.me], ss, rs.at[1 + self.at_end], self.middle)
+        if k == 3:
+            return rcopy(src, dst.at[self.me], ss, rs.at[3], self.sib)
+        if k < 7:
+            j = self.slots[k - 4]
+            return rcopy(dst.at[j], dst.at[j], ss, rs.at[k], self.sib)
+        j = self.slots[k - 6]
+        return rcopy(dst.at[j], dst.at[j], ss, rs.at[k - 6], self.partner)
+
+    def own(self):
+        for k in (1, 0, 3):
+            self.copy(k).start()
+
+    def take(self, kind):
+        j = self.slots[kind]
+        rcopy(
+            self.dst.at[j], self.dst.at[j], self.ss.at[0], self.rs.at[kind], self.partner
+        ).wait_recv()
+        if kind > 0:
+
+            @pl.when(self.at_end == 0)
+            def _():
+                self.copy(6 + kind).start()
+
+        self.copy(4 + kind).start()
+
+    def rest(self):
+        for k in range(3, 7):
+            self.copy(k).wait_recv()
+
+    def sent(self):
+        for k in (0, 1, 3, 4, 5, 6):
+            self.copy(k).wait_send()
+
+        @pl.when(self.at_end == 0)
+        def _():
+            self.copy(7).wait_send()
+            self.copy(8).wait_send()
+
+
+class Scatter:
+    def __init__(self, part, buf, sums, relay, rx, ss, rs):
+        z, m, self.core, f = who()
+        core = self.core
+        partner, middle, end, self.at_end = line_of(z)
+        self.z = z
+        self.part, self.buf, self.sums, self.relay_buf, self.rx = part, buf, sums, relay, rx
+        self.ss, self.rs = ss, rs
+        self.order = [end, middle, partner, z]
+        self.sib = dev(z, m, 1 - core, f)
+        self.to = [dev(zz, m, core, f) for zz in self.order[:3]]
+
+    def sibling(self, i):
+        return rcopy(
+            self.part.at[self.order[i], 1 - self.core],
+            self.buf.at[i],
+            self.ss.at[i],
+            self.rs.at[i],
+            self.sib,
+        )
+
+    def copy(self, i, at_end):
+        if i == 2:
+            return rcopy(
+                self.sums.at[2], self.rx.at[0], self.ss.at[6], self.rs.at[4], self.to[2]
+            )
+        if at_end:
+            return rcopy(
+                self.sums.at[i], self.relay_buf.at[i], self.ss.at[4 + i], self.rs.at[6 + i], self.to[2]
+            )
+        return rcopy(self.sums.at[i], self.rx.at[1], self.ss.at[4 + i], self.rs.at[5], self.to[i])
+
+    def pass_on(self, i):
+        self.sibling(i).wait_recv()
+        self.sums[i] = (
+            self.part[self.order[i], self.core].astype(f32) + self.buf[i].astype(f32)
+        ).astype(bf16)
+        if i == 2:
+            self.copy(2, True).start()
+        else:
+
+            @pl.when(self.at_end == 1)
+            def _():
+                self.copy(i, True).start()
+
+    def relay(self, i):
+        @pl.when(self.at_end == 0)
+        def _():
+            self.copy(i, True).wait_recv()
+            self.sums[i] = (
+                self.sums[i].astype(f32) + self.relay_buf[i].astype(f32)
+            ).astype(bf16)
+            self.copy(i, False).start()
+
+    def total(self):
+        self.sibling(3).wait_recv()
+        total = self.part[self.z, self.core].astype(f32) + self.buf[3].astype(f32)
+        self.copy(2, True).wait_recv()
+        total = total + self.rx[0].astype(f32)
+        self.copy(0, False).wait_recv()
+        return total + self.rx[1].astype(f32)
+
+    def sent(self):
+        for i in range(4):
+            self.sibling(i).wait_send()
+        for i in range(3):
+            self.copy(i, False).wait_send()
+
+
+def scatter_scratch():
+    part = (ROWS, WIDTH)
+    return [
+        pltpu.VMEM((4,) + part, bf16),
+        pltpu.VMEM((3,) + part, bf16),
+        pltpu.VMEM((2,) + part, bf16),
+        pltpu.VMEM((2,) + part, bf16),
+        pltpu.SemaphoreType.DMA((7,)),
+        pltpu.SemaphoreType.DMA((8,)),
+    ]
 
 
 def back_product(left, right):
@@ -235,87 +236,11 @@
     return jnp.where((key >= begin) & (key <= token), e, 0.0)
 
 
-def attend_kernel(span, m_ref, q_ref, kv_ref, begin_ref, sum_ref, tot_ref):
-    m = m_ref[0]
-    for z in range(4):
-        rows = slice(z * BLOCK, (z + 1) * BLOCK)
-        keys = (z + 1) * BLOCK
-        for h in range(2):
-            lanes = slice(h * 64, h * 64 + 64)
-            acc = jnp.zeros((BLOCK, 64), f32)
-            tot = jnp.zeros((BLOCK, 1), f32)
-            q = q_ref[rows, lanes]
-
-            def step(mm, carry):
-                acc, tot = carry
-                e = block_weights(q, kv_ref[mm, :keys, :64], begin_ref[rows, :], z, m, mm, span)
-                acc = acc + dot(e.astype(bf16), kv_ref[mm, :keys, 64:])
-                return acc, tot + jnp.sum(e, axis=1, keepdims=True)
-
-            acc, tot = lax.fori_loop(0, kv_ref.shape[0], step, (acc, tot))
-            sum_ref[rows, lanes] = acc
-            tot_ref[rows, lanes] = jnp.broadcast_to(tot, (BLOCK, 64))
-
-
 VM = pltpu.VMEM
 
 
 def vspecs(n):
     return [pl.BlockSpec(memory_space=VM)] * n
-
-
-def attend(m, q, kv, begin, span):
-    n = q.shape[0]
-    return pl.pallas_call(
-        functools.partial(attend_kernel, span),
-        out_shape=(jax.ShapeDtypeStruct((n, 128), f32), jax.ShapeDtypeStruct((n, 128), f32)),
-        in_specs=[pl.BlockSpec(memory_space=pltpu.SMEM)] + vspecs(3),
-        out_specs=tuple(vspecs(2)),
-        cost_estimate=pl.CostEstimate(flops=2**31, bytes_accessed=2**22, transcendentals=2**22),
-        compiler_params=pltpu.CompilerParams(vmem_limit_bytes=40 * 2**20),
-        name="attend",
-    )(m, q, kv, begin)
-
-
-def attend_back_kernel(span, m_ref, q_ref, kv_ref, begin_ref, g_ref, delta_ref, dq_ref, dkv_ref, acc_ref):
-    m = m_ref[0]
-    dq_ref[...] = jnp.zeros_like(dq_ref)
-
-    def step(mm, _):
-        acc_ref[...] = jnp.zeros_like(acc_ref)
-        for z in range(4):
-            rows = slice(z * BLOCK, (z + 1) * BLOCK)
-            keys = (z + 1) * BLOCK
-            for h in range(2):
-                lanes = slice(h * 64, h * 64 + 64)
-                q = q_ref[rows, lanes]
-                g = g_ref[rows, lanes]
-                k = kv_ref[mm, :keys, :64]
-                v = kv_ref[mm, :keys, 64:]
-                e = block_weights(q, k, begin_ref[rows, :], z, m, mm, span)
-                dp = back_product(g, v)
-                ds = (e * (dp - delta_ref[rows, h * 64 : h * 64 + 1])).astype(bf16)
-                dq_ref[rows, lanes] += dot(ds, k)
-                acc_ref[:keys, :64] += lead_sum(ds, q)
-                acc_ref[:keys, 64:] += lead_sum(e.astype(bf16), g)
-        dkv_ref[mm] = acc_ref[...].astype(dkv_ref.dtype)
-        return 0
-
-    lax.fori_loop(0, kv_ref.shape[0], step, 0)
-
-
-def attend_back(m, q, kv, begin, g, delta, span):
-    n = q.shape[0]
-    return pl.pallas_call(
-        functools.partial(attend_back_kernel, span),
-        out_shape=(jax.ShapeDtypeStruct((n, 128), f32), jax.ShapeDtypeStruct(kv.shape, bf16)),
-        in_specs=[pl.BlockSpec(memory_space=pltpu.SMEM)] + vspecs(5),
-        out_specs=tuple(vspecs(2)),
-        scratch_shapes=[pltpu.VMEM((n, 128), f32)],
-        cost_estimate=pl.CostEstimate(flops=2**33, bytes_accessed=2**23, transcendentals=2**22),
-        compiler_params=pltpu.CompilerParams(vmem_limit_bytes=48 * 2**20),
-        name="attend_back",
-    )(m, q, kv, begin, g, delta)
 
 
 def begin_of(token, doc_ref):
@@ -367,22 +292,9 @@
 
     enter([sib, pair] + zpeers + mpeers)
 
-    def gather(src, dst, ss, rs, k):
-        if k < 3:
-            return rcopy(src, dst.at[me], ss.at[k], rs.at[k], zpeers[k])
-        if k == 3:
-            return rcopy(src, dst.at[me], ss.at[k], rs.at[k], sib)
-        j = slot((z + 3 - (k - 4)) % 4, core)
-        return rcopy(dst.at[j], dst.at[j], ss.at[k], rs.at[k], sib)
-
-    def x_copy(k):
-        return gather(x_ref, x_all, s_x, r_x, k)
-
-    def c_copy(k):
-        return gather(c_ref, c_all, s_c, r_c, k)
-
-    for k in (1, 0, 2, 3):
-        x_copy(k).start()
+    gx = Gather(x_ref, x_all, s_x, r_x)
+    gc = Gather(c_ref, c_all, s_c, r_c)
+    gx.own()
     head_rows = pl.ds(f * half_width, half_width)
     heads_copy = rcopy(wh_ref, w_heads.at[head_rows], s_h.at[0], r_h.at[0], pair)
     heads_copy.start()
@@ -406,9 +318,6 @@
         place = w_out.at[pl.ds(pl.multiple_of(part * eighth, 8), eighth)]
         return rcopy(place, place, s_o.at[k], r_o.at[k], sib)
 
-    for k in (0, 1, 3):
-        w_copy(k, 0).start()
-
     @pl.when(owner)
     def _():
         w_copy(2, 0).start()
@@ -433,11 +342,11 @@
         return 0
 
     lax.fori_loop(0, 4, table, 0)
-    for k in range(3):
-        x_copy(k).wait_recv()
-        x_copy(k + 4).start()
-    for k in (1, 0, 2, 3):
-        c_copy(k).start()
+    for k in (0, 1, 3):
+        w_copy(k, 0).start()
+    for kind in (0, 1, 2):
+        gx.take(kind)
+    gc.own()
     heads_copy.wait_recv()
 
     def kv_copy(b, s):
@@ -449,8 +358,7 @@
     qgain = qgain_ref[...]
     kgain = kgain_ref[...]
 
-    for k in range(3, 7):
-        x_copy(k).wait_recv()
+    gx.rest()
 
     def project(b, _):
         rows = pl.ds(pl.multiple_of(b * BLOCK, BLOCK), BLOCK)
@@ -475,9 +383,14 @@
         return 0
 
     lax.fori_loop(0, 4, project, 0)
-    for k in range(2):
-        w_copy(k, 0).wait_recv()
-        w_copy(k, 1).start()
+
+    @pl.when(jnp.logical_not(owner))
+    def _():
+        w_copy(2, 0).wait_recv()
+        w_copy(2, 1).start()
+
+    w_copy(0, 0).wait_recv()
+    w_copy(0, 1).start()
 
     summed[...] = jnp.zeros_like(summed)
     totals[...] = jnp.zeros_like(totals)
@@ -491,6 +404,14 @@
                 rows = pl.ds(b * BLOCK, BLOCK)
                 place = kv_all.at[mm, rows]
                 rcopy(place, place, s_k.at[b, s - 1], r_k.at[b, s - 1], sib).wait_recv()
+
+        @pl.when(s == 1)
+        def _():
+            w_copy(1, 0).wait_recv()
+            w_copy(1, 1).start()
+            w_copy(3, 0).wait_recv()
+            w_copy(3, 1).start()
+            out_copy(0).start()
 
         for zz in range(4):
             rows = slice(zz * BLOCK, (zz + 1) * BLOCK)
@@ -512,18 +433,8 @@
         rows = slice(b * BLOCK, (b + 1) * BLOCK)
         att[b] = (summed[rows, :] / totals[rows, :]).astype(bf16)
 
-    w_copy(3, 0).wait_recv()
-    w_copy(3, 1).start()
-    out_copy(0).start()
-
-    @pl.when(jnp.logical_not(owner))
-    def _():
-        w_copy(2, 0).wait_recv()
-        w_copy(2, 1).start()
-
-    for k in range(3):
-        c_copy(k).wait_recv()
-        c_copy(k + 4).start()
+    for kind in (0, 1, 2):
+        gc.take(kind)
 
     def w_got(k):
         dst = (w_gate, w_up, w_down, w_out)[k]
@@ -546,15 +457,13 @@
     def _():
         w_copy(2, 0).wait_send()
 
-    for k in range(3, 7):
-        c_copy(k).wait_recv()
+    gc.rest()
     for k in range(2):
         out_copy(k).wait_recv()
     stay.wait()
     heads_copy.wait_send()
-    for k in range(7):
-        x_copy(k).wait_send()
-        c_copy(k).wait_send()
+    gx.sent()
+    gc.sent()
     for k in (0, 1, 3):
         w_copy(k, 0).wait_send()
         w_copy(k, 1).wait_send()
@@ -596,7 +505,7 @@
         + vspecs(3) + any_specs(4) + vspecs(3),
         out_specs=tuple(vspecs(1) + any_specs(1) + vspecs(1) + any_specs(4) + vspecs(9)),
         scratch_shapes=[
-            sem((7,)), sem((7,)), sem((7,)), sem((7,)), sem((1,)), sem((1,)),
+            sem((9,)), sem((7,)), sem((9,)), sem((7,)), sem((1,)), sem((1,)),
             sem((4,)), sem((4,)), sem((4,)), sem((4,)), sem((2,)), sem((2,)),
             sem((4, M - 1)), sem((4, M - 1)), sem((5,)),
         ],
@@ -610,15 +519,16 @@
 def ffn_kernel(
     att_ref, x_hbm, c_hbm, own_c_ref, wo_own, wg_own, wu_own, wd_own, wo_got, wg_got, wu_got, wd_got,
     gain_ref,
-    att_all, branch_ref, gmid_ref, mid_ref, dpart_ref, gpart_ref, glu_rx, down_rx,
-    x_v, c_v, wo_v, wg_v, wu_v, wd_v, normed, hid, gg, gu, mid_b, p_out, p_sib, p_sum, p_rx,
-    glu_tx, down_tx, br_own,
-    ld, s_att, r_att, s_sib, r_sib, s_rs, r_rs, s_br, r_br, s_x, r_x, l_x,
+    att_all, branch_ref, gmid_ref, mid_ref, dpart_ref, gpart_ref, gate_rx, down_rx, up_tx,
+    x_v, c_v, wo_v, wg_v, wu_v, wd_v, normed, hid, gg, gu, mid_b, p_out,
+    p_sib, p_sum, p_relay, p_rx, s_rs, r_rs,
+    gate_tx, down_tx, br_own,
+    ld, s_att, r_att, s_pass, s_sib, r_sib, s_br, r_br, s_x, r_x, l_x,
 ):
     z, m, core, f = who()
     M = lax.axis_size("ctx") // 8
     T = 2 * M
-    seg = glu_tx.shape[2]
+    seg = gate_tx.shape[1]
     each = WIDTH // lax.axis_size("ctx")
     half_width = WIDTH // 2
     sib = dev(z, m, 1 - core, f)
@@ -665,61 +575,66 @@
 
     me = slot(z, core)
 
-    def send_att(s, i):
-        b = (zs[s] + 1 + i) % 4
-        return rcopy(
-            att_ref.at[b], att_all.at[b, :, lanes(me)], s_att.at[s, i], r_att.at[s, i], zpeers[s]
-        )
-
-    def got_att(s, i):
-        b = (z + 1 + i) % 4
-        j = slot((z + 3 - s) % 4, core)
-        return rcopy(
-            att_ref.at[b], att_all.at[b, :, lanes(j)], s_att.at[s, i], r_att.at[s, i], zpeers[s]
-        )
+    partner, middle, end, at_end = line_of(z)
+    order = [end, middle, partner, z]
+    to_partner = [end, middle, z, partner]
+    to_middle = [3 * (z // 2), 1 + z // 2, end, middle]
+    from_slot = [slot(zz, core) for zz in (partner, middle, end)]
+    to_p, to_m = dev(partner, m, core, f), dev(middle, m, core, f)
+
+    def att_copy(k, i):
+        if k == 0:
+            b = to_partner[i]
+            return rcopy(
+                att_ref.at[b], att_all.at[b, :, lanes(me)], s_att.at[0, i], r_att.at[0, i], to_p
+            )
+        if k == 1:
+            b = to_middle[i]
+            return rcopy(
+                att_ref.at[b],
+                att_all.at[b, :, lanes(me)],
+                s_att.at[1, i],
+                r_att.at[1 + at_end, i],
+                to_m,
+            )
+        place = att_all.at[order[i], :, lanes(from_slot[k - 1])]
+        return rcopy(place, place, s_pass.at[k - 2, i], r_att.at[k - 1, (0, 1, 3, 2)[i]], to_p)
 
     def sib_att(k, i):
-        b = (z + 1 + i) % 4
-        j = me if k == 3 else slot((z + 3 - k) % 4, core)
+        b = order[i]
+        j = me if k == 3 else from_slot[k]
         src = att_ref.at[b] if k == 3 else att_all.at[b, :, lanes(j)]
         return rcopy(src, att_all.at[b, :, lanes(j)], s_sib.at[k, i], r_sib.at[k, i], sib)
 
-    def from_sib(k, i):
-        b = (z + 1 + i) % 4
-        j = slot(z, 1 - core) if k == 3 else slot((z + 3 - k) % 4, 1 - core)
-        return rcopy(att_ref.at[b], att_all.at[b, :, lanes(j)], s_sib.at[k, i], r_sib.at[k, i], sib)
-
     for i in range(4):
-        for s in (1, 0, 2):
-            send_att(s, i).start()
+        att_copy(1, i).start()
+        att_copy(0, i).start()
         sib_att(3, i).start()
     for b in range(4):
         att_all[b, :, lanes(me)] = att_ref[b]
 
     def forward(i):
-        for s in range(3):
-            got_att(s, i).wait_recv()
-            sib_att(s, i).start()
-
-    def p_copy(i):
-        return rcopy(p_out.at[i, 1 - core], p_sib.at[i], s_rs.at[i], r_rs.at[i], sib)
-
-    def rs_copy(i):
-        return rcopy(p_sum.at[i], p_rx.at[i], s_rs.at[4 + i], r_rs.at[4 + i], zpeers[i])
-
-    def reduce_block(i):
-        p_copy(i).wait_recv()
-        p_sum[i] = (p_out[i, core].astype(f32) + p_sib[i].astype(f32)).astype(bf16)
-        rs_copy(i).start()
+        for k in range(3):
+            place = att_all.at[order[i], :, lanes(from_slot[k])]
+            rcopy(place, place, s_att.at[0, i], r_att.at[k, i], to_p).wait_recv()
+            if k > 0:
+
+                @pl.when(at_end == 0)
+                def _(k=k):
+                    att_copy(k + 1, i).start()
+
+            sib_att(k, i).start()
+
+    sc = Scatter(p_out, p_sib, p_sum, p_relay, p_rx, s_rs, r_rs)
 
     forward(0)
     gain = gain_ref[...]
     for cp in loads:
         cp.wait()
     for i in range(4):
-        b = (z + 1 + i) % 4
+        b = order[i]
         for k in range(4):
-            from_sib(k, i).wait_recv()
+            sib_att(k, i).wait_recv()
         mid = x_v[b].astype(f32) + dot(att_all[b], wo_v[...])
         nb = (
             mid * lax.rsqrt(jnp.mean(mid * mid, axis=-1, keepdims=True) + epsilon) * gain
@@ -728,8 +643,8 @@
         if i == 3:
             mid_b[0] = mid[:ROWS]
             mid_b[1] = mid[ROWS:]
-        if i < 3:
-            forward(i + 1)
+        for ii in ((1,), (2, 3), (), ())[i]:
+            forward(ii)
         gate = dot(nb, wg_v[...])
         up = dot(nb, wu_v[...])
         sig = 1.0 / (1.0 + jnp.exp(-gate))
@@ -742,43 +657,42 @@
         gg[b] = ggb
         gu[b] = gub
         pb = (back_product(ggb, wg_v[...]) + back_product(gub, wu_v[...])).astype(bf16)
-        p_out[i, 0] = pb[:ROWS]
-        p_out[i, 1] = pb[ROWS:]
-        p_copy(i).start()
+        p_out[b, 0] = pb[:ROWS]
+        p_out[b, 1] = pb[ROWS:]
+        sc.sibling(i).start()
         if i > 0:
-            reduce_block(i - 1)
+            sc.pass_on(i - 1)
+        if i > 1:
+            sc.relay(i - 2)
         db = dot(hb, wd_v[...]).astype(bf16)
         dpart_ref[b, 0] = db[:ROWS]
         dpart_ref[b, 1] = db[ROWS:]
 
     def x_copy(which, s):
-        tx, rx = (glu_tx, glu_rx) if which < 2 else (down_tx, down_rx)
-        if which < 2:
-            src, dst = tx.at[others[s], which], rx.at[group, which]
-        else:
-            src, dst = tx.at[others[s]], rx.at[group]
-        return rcopy(src, dst, s_x.at[which, s], r_x.at[which, s], tpeers[s])
+        tx, rx = ((gate_tx, gate_rx), (down_tx, down_rx))[which]
+        return rcopy(
+            tx.at[others[s]], rx.at[group], s_x.at[which, s], r_x.at[which, s], tpeers[s]
+        )
 
     def x_own(which):
-        if which < 2:
-            return pltpu.make_async_copy(
-                glu_tx.at[group, which], glu_rx.at[group, which], l_x.at[which]
-            )
-        return pltpu.make_async_copy(down_tx.at[group], down_rx.at[group], l_x.at[which])
-
-    def flat(ref):
-        return ref[...].reshape(8 * ROWS, ref.shape[-1])
-
-    def glu_grads(which):
-        prod = lead_sum(flat((gg, gu)[which]), flat(normed)).astype(bf16)
-        for mm in range(M):
-            for ff in range(2):
-                glu_tx[mm * 2 + ff, which] = prod[
-                    mm * seg : (mm + 1) * seg, ff * half_width : (ff + 1) * half_width
-                ]
+        tx, rx = ((gate_tx, gate_rx), (down_tx, down_rx))[which]
+        return pltpu.make_async_copy(tx.at[group], rx.at[group], l_x.at[which])
+
+    def send_grads(which):
         for s in range(T - 1):
             x_copy(which, s).start()
         x_own(which).start()
+
+    def flat(ref):
+        return ref[...].reshape(8 * ROWS, ref.shape[-1])
+
+    def glu_grads(grads, tx):
+        prod = lead_sum(flat(grads), flat(normed)).astype(bf16)
+        for mm in range(M):
+            for ff in range(2):
+                tx[mm * 2 + ff] = prod[
+                    mm * seg : (mm + 1) * seg, ff * half_width : (ff + 1) * half_width
+                ]
 
     def down_grads():
         prod = lead_sum(flat(hid), flat(c_v))
@@ -789,21 +703,16 @@
                         prod[:, blk * each : (blk + 1) * each]
                         for zl in range(2)
                         for cc in range(2)
-                        for blk in [(2 * ff + zl) * 2 * M + mm * 2 + cc]
+                        for blk in [(2 * zl + ff) * 2 * M + mm * 2 + cc]
                     ],
                     axis=1,
                 ).astype(bf16)
-        for s in range(T - 1):
-            x_copy(2, s).start()
-        x_own(2).start()
-
-    glu_grads(0)
-
-    p_copy(3).wait_recv()
-    dy = p_out[3, core].astype(f32) + p_sib[3].astype(f32)
-    for i in range(3):
-        rs_copy(i).wait_recv()
-        dy = dy + p_rx[i].astype(f32)
+    down_grads()
+    send_grads(1)
+    glu_grads(gg, gate_tx)
+    send_grads(0)
+
+    dy = sc.total()
     mid = mid_b[core]
     r = lax.rsqrt(jnp.mean(mid * mid, axis=-1, keepdims=True) + epsilon)
     gdy = gain * dy
@@ -815,38 +724,30 @@
     br_own[...] = gmid.astype(bf16)
     branch_ref[me] = br_own[...]
 
-    def br_copy(k):
-        if k < 3:
-            return rcopy(br_own, branch_ref.at[me], s_br.at[k], r_br.at[k], zpeers[k])
-        j = me if k == 3 else slot((z + 3 - (k - 4)) % 4, core)
-        return rcopy(
-            br_own if k == 3 else branch_ref.at[j], branch_ref.at[j], s_br.at[k], r_br.at[k], sib
-        )
-
-    for k in (1, 0, 2, 3):
-        br_copy(k).start()
-    glu_grads(1)
-    down_grads()
-    for k in range(3):
-        br_copy(k).wait_recv()
-        br_copy(k + 4).start()
-    for k in range(3, 7):
-        br_copy(k).wait_recv()
-    for which in range(3):
+    gb = Gather(br_own, branch_ref, s_br, r_br)
+    gb.own()
+    glu_grads(gu, up_tx)
+    for kind in (0, 1, 2):
+        gb.take(kind)
+    gb.rest()
+    for which in range(2):
         x_own(which).wait()
         for s in range(T - 1):
             x_copy(which, s).wait_recv()
     for i in range(4):
-        for s in range(3):
-            send_att(s, i).wait_send()
+        for k in range(2):
+            att_copy(k, i).wait_send()
         for k in range(4):
             sib_att(k, i).wait_send()
-        p_copy(i).wait_send()
-    for i in range(3):
-        rs_copy(i).wait_send()
-    for k in range(7):
-        br_copy(k).wait_send()
-    for which in range(3):
+
+        @pl.when(at_end == 0)
+        def _(i=i):
+            att_copy(2, i).wait_send()
+            att_copy(3, i).wait_send()
+
+    sc.sent()
+    gb.sent()
+    for which in range(2):
         for s in range(T - 1):
             x_copy(which, s).wait_send()
 
@@ -867,11 +768,12 @@
             shape((ROWS, WIDTH), f32),
             shape((4, 2, ROWS, WIDTH), bf16),
             shape((1, WIDTH), f32),
-            shape((T, 2, seg, half_width), bf16),
+            shape((T, seg, half_width), bf16),
             shape((T, cols, 4 * each), bf16),
+            shape((T, seg, half_width), bf16),
         ),
         in_specs=vspecs(1) + any_specs(2) + vspecs(1) + any_specs(8) + vspecs(1),
-        out_specs=tuple(vspecs(8)),
+        out_specs=tuple(vspecs(9)),
         scratch_shapes=[
             VS((4, BLOCK, WIDTH), bf16),
             VS((4, BLOCK, WIDTH), bf16),
@@ -885,24 +787,21 @@
             VS((4, BLOCK, cols), bf16),
             VS((2, ROWS, WIDTH), f32),
             VS((4, 2, ROWS, WIDTH), bf16),
-            VS((4, ROWS, WIDTH), bf16),
-            VS((3, ROWS, WIDTH), bf16),
-            VS((3, ROWS, WIDTH), bf16),
-            VS((T, 2, seg, half_width), bf16),
+            *scatter_scratch(),
+            VS((T, seg, half_width), bf16),
             VS((T, cols, 4 * each), bf16),
             VS((ROWS, WIDTH), bf16),
             sem((9,)),
+            sem((2, 4)),
             sem((3, 4)),
-            sem((3, 4)),
+            sem((2, 4)),
             sem((4, 4)),
             sem((4, 4)),
+            sem((9,)),
             sem((7,)),
-            sem((7,)),
-            sem((7,)),
-            sem((7,)),
-            sem((3, T - 1)),
-            sem((3, T - 1)),
-            sem((3,)),
+            sem((2, T - 1)),
+            sem((2, T - 1)),
+            sem((2,)),
         ],
         compiler_params=pltpu.CompilerParams(
             collective_id=cid, has_side_effects=True, vmem_limit_bytes=60 * 2**20
@@ -913,11 +812,13 @@
 
 def back_kernel(
     doc_ref, branch_ref, att_ref, wo_own, wo_got, q_rows, kv_all, summed, totals, stacked, cosine, sine,
-    normed, w_heads, dpart, mid_ref, gmid_ref, x_ref, again_ref, qgain_ref, kgain_ref, fpart_ref,
-    out_ref, igrad_ref, gains_ref, heads_ref, attn_ref,
+    normed, w_heads, dpart, mid_ref, gmid_ref, x_ref, x_all, again_ref, qgain_ref, kgain_ref, fpart_ref,
+    gate_rx, down_rx, up_tx,
+    out_ref, igrad_ref, gains_ref, heads_ref, attn_ref, gate_ref, up_ref, down_ref,
     wo_v, g_v, delta_v, dq_v, dkv_acc, dkv_tx, dkv_rx, gs_v,
-    d_sib, d_sum, d_rx, p_part, p_sib, p_sum, p_rx, h_tx, h_rx, a_tx, a_rx, gn_tx, gn_rx, gt_tx, gt_rx,
-    ld, s_d, r_d, s_p, r_p, s_k, r_k, s_h, r_h, l_h, s_a, r_a, l_a, s_g, r_g, s_t, r_t,
+    d_sib, d_sum, d_relay, d_rx, s_d, r_d, p_sib, p_sum, p_relay, p_rx, s_p, r_p, p_part,
+    h_tx, h_rx, a_tx, a_rx, gn_tx, gn_rx, gt_tx, gt_rx, up_rx, w_tx, w_rx,
+    ld, s_k, r_k, s_h, r_h, l_h, s_a, r_a, l_a, s_g, r_g, s_t, r_t, s_u, r_u, s_w, r_w,
 ):
     z, m, core, f = who()
     M = lax.axis_size("ctx") // 8
@@ -972,32 +873,36 @@
         def _(s=s):
             pl.semaphore_signal(bar, inc=1, device_id=piece_from[s], device_id_type=MESH)
 
-    pl.semaphore_wait(bar, len(fixed) + T - jnp.where(core_from == core, 1, 0))
-
-    def sib_copy(part, buf, ss, rs, i):
-        b = (z + 1 + i) % 4
-        return rcopy(part.at[b, 1 - core], buf.at[i], ss.at[i], rs.at[i], sib)
-
-    def z_copy(sums, rx, ss, rs, i):
-        return rcopy(sums.at[i], rx.at[i], ss.at[4 + i], rs.at[4 + i], zpeers[i])
-
-    def pass_on(part, buf, sums, rx, ss, rs, i):
-        sib_copy(part, buf, ss, rs, i).wait_recv()
-        b = (z + 1 + i) % 4
-        sums[i] = (part[b, core].astype(f32) + buf[i].astype(f32)).astype(bf16)
-        z_copy(sums, rx, ss, rs, i).start()
-
-    def total_of(part, buf, rx, sums, ss, rs):
-        sib_copy(part, buf, ss, rs, 3).wait_recv()
-        total = part[z, core].astype(f32) + buf[3].astype(f32)
-        for i in range(3):
-            z_copy(sums, rx, ss, rs, i).wait_recv()
-            total = total + rx[i].astype(f32)
-        return total
-
-    D = (dpart, d_sib, d_sum, d_rx, s_d, r_d)
+    place = [(zl, cc) for zl in range(2) for cc in range(2)]
+    place_dev = [dev(2 * zl + f, m, cc, z // 2) for zl, cc in place]
+    place_self = [owner & (z == 2 * zl + f) & (core == cc) for zl, cc in place]
+    place_from = [dev(2 * f + zb, m, cc, z % 2) for zb, cc in place]
+    from_me = [owner & (z == 2 * f + zb) & (z % 2 == f) & (core == cc) for zb, cc in place]
+    for k in range(4):
+
+        @pl.when(jnp.logical_not(from_me[k]))
+        def _(k=k):
+            pl.semaphore_signal(bar, inc=1, device_id=place_from[k], device_id_type=MESH)
+
+    pl.semaphore_wait(
+        bar,
+        len(fixed)
+        + T
+        + 4
+        - jnp.where(core_from == core, 1, 0)
+        - jnp.where(owner & (z % 2 == f), 1, 0),
+    )
+
+    sd = Scatter(dpart, d_sib, d_sum, d_relay, d_rx, s_d, r_d)
+    sp = Scatter(p_part, p_sib, p_sum, p_relay, p_rx, s_p, r_p)
     for i in range(4):
-        sib_copy(dpart, d_sib, s_d, r_d, i).start()
+        sd.sibling(i).start()
+
+    def u_copy(s):
+        return rcopy(up_tx.at[others[s]], up_rx.at[group], s_u.at[s], r_u.at[s], tpeers[s])
+
+    for s in range(T - 1):
+        u_copy(s).start()
 
     @pl.when(owner)
     def _():
@@ -1025,7 +930,30 @@
 
     lax.fori_loop(0, 4, mixed, 0)
     for i in range(3):
-        pass_on(*D[:4], s_d, r_d, i)
+        sd.pass_on(i)
+
+    total = down_rx[0].astype(f32)
+    for k in range(1, T):
+        total = total + down_rx[k].astype(f32)
+    for k in range(4):
+        w_tx[k] = packed(total[:, k * each : (k + 1) * each]).astype(bf16)
+    here = z % 2 * 2 + core
+
+    def w_copy(k):
+        return rcopy(w_tx.at[k], w_rx.at[here], s_w.at[k], r_w.at[here], place_dev[k])
+
+    for k in range(4):
+
+        @pl.when(jnp.logical_not(place_self[k]))
+        def _(k=k):
+            w_copy(k).start()
+
+        @pl.when(place_self[k])
+        def _(k=k):
+            w_rx[here] = w_tx[k]
+
+    for i in range(2):
+        sd.relay(i)
 
     dq_v[...] = jnp.zeros_like(dq_v)
 
@@ -1067,6 +995,14 @@
 
     lax.fori_loop(0, M, attend, 0)
 
+    def over_groups(rx):
+        total = rx[0].astype(f32)
+        for k in range(1, T):
+            total = total + rx[k].astype(f32)
+        return total
+
+    gate_ref[...] = jnp.transpose(over_groups(gate_rx))
+
     strip = jnp.concatenate(
         [branch_ref[j, :, pl.ds(pl.multiple_of(z * 256, 128), 256)] for j in range(8)], axis=0
     )
@@ -1084,9 +1020,9 @@
     prod = lead_sum(att_ref[...].reshape(8 * ROWS, WIDTH), strip).astype(bf16)
     for mm in range(M):
         for ff in range(2):
-            a_tx[mm * 2 + ff] = prod[
-                ff * half_width : (ff + 1) * half_width, mm * each : (mm + 1) * each
-            ]
+            a_tx[mm * 2 + ff] = packed(
+                prod[ff * half_width : (ff + 1) * half_width, mm * each : (mm + 1) * each]
+            )
 
     def a_copy(s):
         return rcopy(a_tx.at[others[s]], a_rx.at[group], s_a.at[s], r_a.at[s], tpeers[s])
@@ -1108,8 +1044,8 @@
         return jnp.where(low, a, c) * (1.0 / 64)
 
     def heads_back(i, carry):
-        qg, kg = carry
-        b = (z + 1 + i) % 4
+        qg, kg, ag = carry
+        b = jnp.where(i == 0, sp.order[0], jnp.where(i == 1, sp.order[1], jnp.where(i == 2, sp.order[2], z)))
         rows = block_rows(b)
         co = cosine[rows, :]
         si = sine[rows, :]
@@ -1130,16 +1066,38 @@
         low = lax.broadcasted_iota(jnp.int32, dkv.shape, 1) < 64
         gs = jnp.concatenate([dq, jnp.where(low, dk, dkv)], axis=1).astype(bf16)
         gs_v[rows, :] = gs
-        pb = back_product(gs, w_heads[...]).astype(bf16)
+        pb = back_product(gs, w_heads[...])
+        xb = jnp.concatenate([x_all[2 * b], x_all[2 * b + 1]], axis=0).astype(f32)
+        rb = lax.rsqrt(jnp.mean(xb * xb, axis=-1, keepdims=True) + epsilon)
+        ag = ag + jnp.sum(pb * (xb * rb), axis=0, keepdims=True)
+        pb = pb.astype(bf16)
         p_part[b, 0] = pb[:ROWS]
         p_part[b, 1] = pb[ROWS:]
-        sib_copy(p_part, p_sib, s_p, r_p, i).start()
-        return qg + qpart, kg + kpart
+        rcopy(
+            p_part.at[b, 1 - core], p_sib.at[i], s_p.at[i], r_p.at[i], sib
+        ).start()
+        return qg + qpart, kg + kpart, ag
 
     zero = jnp.zeros((1, 128), f32)
-    qg, kg = lax.fori_loop(0, 4, heads_back, (zero, zero))
+    qg, kg, ag = lax.fori_loop(
+        0, 4, heads_back, (zero, zero, jnp.zeros((1, WIDTH), f32))
+    )
     for i in range(3):
-        pass_on(p_part, p_sib, p_sum, p_rx, s_p, r_p, i)
+        sp.pass_on(i)
+
+    def stack(row):
+        return jnp.concatenate([row[:, k * 128 : (k + 1) * 128] for k in range(8)], axis=0)
+
+    gn_tx[0:8, :] = stack(ag)
+    gn_tx[8:16, :] = stack(fpart_ref[...])
+    gn_tx[16:24, :] = jnp.concatenate([qg, kg, jnp.zeros((6, 128), f32)], axis=0)
+    gpeers = [sib] + zpeers + cross
+
+    def g_copy(k):
+        return rcopy(gn_tx, gn_rx.at[k], s_g.at[k], r_g.at[k], gpeers[k])
+
+    for k in range(7):
+        g_copy(k).start()
 
     prod = lead_sum(normed[...], gs_v[...]).astype(bf16)
     qw, kw = 128 // M, 64 // M
@@ -1178,38 +1136,48 @@
         def _(s=s):
             h_copy(s).start()
 
-    out_ref[...] = mid_ref[...] + total_of(dpart, d_sib, d_rx, d_sum, s_d, r_d)
-    dy = total_of(p_part, p_sib, p_rx, p_sum, s_p, r_p)
+    for i in range(2):
+        sp.relay(i)
+    gains = gn_tx[...]
+    for k in range(7):
+        g_copy(k).wait_recv()
+    for k in range(7):
+        gains = gains + gn_rx[k]
+    gt_tx[...] = gains
+
+    def t_copy(s):
+        return rcopy(gt_tx, gt_rx.at[s], s_t.at[s], r_t.at[s], tpeers[s])
+
+    for s in range(T - 1):
+        t_copy(s).start()
+
+
+    for s in range(T - 1):
+        u_copy(s).wait_recv()
+    up_rx[group] = up_tx[group]
+    up_ref[...] = jnp.transpose(over_groups(up_rx))
+    for k in range(4):
+
+        @pl.when(jnp.logical_not(from_me[k]))
+        def _(k=k):
+            rcopy(w_tx.at[k], w_rx.at[k], s_w.at[k], r_w.at[k], place_from[k]).wait_recv()
+
+    seg = gate_rx.shape[1]
+    for zl in range(2):
+        for cc in range(2):
+            for mm in range(M):
+                at = ((zl * M + mm) * 2 + cc) * seg
+                down_ref[at : at + seg, :] = w_rx[
+                    zl * 2 + cc, :, mm * each : (mm + 1) * each
+                ].astype(f32)
+
+    out_ref[...] = mid_ref[...] + sd.total()
+    dy = sp.total()
     x = x_ref[...].astype(f32)
     r = lax.rsqrt(jnp.mean(x * x, axis=-1, keepdims=True) + epsilon)
     gdy = again_ref[...] * dy
     dv = r * gdy - x * (r * r * r) * jnp.mean(x * gdy, axis=-1, keepdims=True)
     igrad_ref[...] = gmid_ref[...] + dv
-
-    gn_tx[0:1, :] = jnp.sum(dy * x * r, axis=0, keepdims=True)
-    gn_tx[1:2, :] = fpart_ref[...]
-    gn_tx[2:3, :] = jnp.concatenate(
-        [qg, kg, jnp.zeros((1, WIDTH - 256), f32)], axis=1
-    )
-    gpeers = [sib] + zpeers + cross
-
-    def g_copy(k):
-        return rcopy(gn_tx, gn_rx.at[k], s_g.at[k], r_g.at[k], gpeers[k])
-
-    for k in range(7):
-        g_copy(k).start()
-    total = gn_tx[...]
-    for k in range(7):
-        g_copy(k).wait_recv()
-    for k in range(7):
-        total = total + gn_rx[k]
-    gt_tx[...] = total
-
-    def t_copy(s):
-        return rcopy(gt_tx, gt_rx.at[s], s_t.at[s], r_t.at[s], tpeers[s])
-
-    for s in range(T - 1):
-        t_copy(s).start()
 
     for s in range(T):
 
@@ -1230,19 +1198,25 @@
         hsum = hsum + h_rx[k].astype(f32)
         asum = asum + a_rx[k].astype(f32)
     heads_ref[...] = hsum
-    attn_ref[...] = asum
+    size = asum.shape[0]
+    for g in range(128 // each):
+        attn_ref[g * size : (g + 1) * size, :] = asum[:, g * each : (g + 1) * each]
 
     for s in range(T - 1):
         t_copy(s).wait_recv()
-        total = total + gt_rx[s]
-    gains_ref[...] = total
-
-    for i in range(4):
-        sib_copy(dpart, d_sib, s_d, r_d, i).wait_send()
-        sib_copy(p_part, p_sib, s_p, r_p, i).wait_send()
-    for i in range(3):
-        z_copy(d_sum, d_rx, s_d, r_d, i).wait_send()
-        z_copy(p_sum, p_rx, s_p, r_p, i).wait_send()
+        gains = gains + gt_rx[s]
+    gains_ref[...] = gains
+
+    sd.sent()
+    sp.sent()
+    for k in range(4):
+
+        @pl.when(jnp.logical_not(place_self[k]))
+        def _(k=k):
+            w_copy(k).wait_send()
+
+    for s in range(T - 1):
+        u_copy(s).wait_send()
     for s in range(M - 1):
         kv_copy(s).wait_send()
     for s in range(T):
@@ -1271,12 +1245,15 @@
         out_shape=(
             shape(part, f32),
             shape(part, f32),
-            shape((3, WIDTH), f32),
+            shape((24, 128), f32),
             shape((half_width, 256 // M), f32),
             shape((half_width, each), f32),
+            shape((half_width, FF // n), f32),
+            shape((half_width, FF // n), f32),
+            shape((FF // 2, each), f32),
         ),
-        in_specs=[pl.BlockSpec(memory_space=pltpu.SMEM)] + vspecs(2) + any_specs(2) + vspecs(17),
-        out_specs=tuple(vspecs(5)),
+        in_specs=[pl.BlockSpec(memory_space=pltpu.SMEM)] + vspecs(2) + any_specs(2) + vspecs(21),
+        out_specs=tuple(vspecs(8)),
         scratch_shapes=[
             VS((128, WIDTH), bf16),
             VS((tokens, 128), bf16),
@@ -1286,28 +1263,28 @@
             VS((M - 1, tokens, 128), bf16),
             VS((M - 1, tokens, 128), bf16),
             VS((tokens, 256), bf16),
-            VS((4,) + part, bf16),
-            VS((3,) + part, bf16),
-            VS((3,) + part, bf16),
+            *scatter_scratch(),
+            *scatter_scratch(),
             VS((4, 2) + part, bf16),
-            VS((4,) + part, bf16),
-            VS((3,) + part, bf16),
-            VS((3,) + part, bf16),
             VS((T, half_width, 256 // M), bf16),
             VS((T, half_width, 256 // M), bf16),
-            VS((T, half_width, each), bf16),
-            VS((T, half_width, each), bf16),
-            VS((3, WIDTH), f32),
-            VS((7, 3, WIDTH), f32),
-            VS((3, WIDTH), f32),
-            VS((T - 1, 3, WIDTH), f32),
+            VS((T, half_width * each // 128, 128), bf16),
+            VS((T, half_width * each // 128, 128), bf16),
+            VS((24, 128), f32),
+            VS((7, 24, 128), f32),
+            VS((24, 128), f32),
+            VS((T - 1, 24, 128), f32),
+            VS((T, FF // n, half_width), bf16),
+            VS((4, FF // 8 * each // 128, 128), bf16),
+            VS((4, FF // 8 * each // 128, 128), bf16),
             sem((1,)),
-            sem((7,)), sem((7,)), sem((7,)), sem((7,)),
             sem((M - 1,)), sem((M - 1,)),
             sem((T,)), sem((T,)), sem((1,)),
             sem((T - 1,)), sem((T - 1,)), sem((1,)),
             sem((7,)), sem((7,)),
             sem((T - 1,)), sem((T - 1,)),
+            sem((T - 1,)), sem((T - 1,)),
+            sem((4,)), sem((4,)),
         ],
         compiler_params=pltpu.CompilerParams(
             collective_id=cid, has_side_effects=True, vmem_limit_bytes=60 * 2**20
@@ -1420,7 +1397,7 @@
         k_gain,
         1,
     )
-    attended, branch, grad_middle, own, down_parts, ffn_gain_part, glu_got, down_got = feed_forward(
+    attended, branch, grad_middle, own, down_parts, ffn_gain_part, gate_got, down_got, up_give = feed_forward(
         att_own,
         x_rows.reshape(4, BLOCK, WIDTH),
         c_rows.reshape(4, BLOCK, WIDTH),
@@ -1430,7 +1407,7 @@
         ffn_gain[None],
         4,
     )
-    output, input_grad, gains, heads_grad, attn_grad = back(
+    output, input_grad, gains, heads_grad, attn_grad, gate_grad, up_grad, down_grad = back(
         doc_lengths,
         branch,
         attended,
@@ -1449,43 +1426,16 @@
         own,
         grad_middle,
         hidden_in[0],
+        x_rows,
         attn_gain[None],
         q_gain,
         k_gain,
         ffn_gain_part,
+        gate_got,
+        down_got,
+        up_give,
         cid=7,
     )
-
-    glu_grad = jnp.sum(glu_got.astype(f32), axis=0)
-    down_sum = jnp.sum(down_got.astype(f32), axis=0)
-    gate_grad = jnp.transpose(glu_grad[0])
-    up_grad = jnp.transpose(glu_grad[1])
-
-    devices = [
-        (zz, mm, cc, ff) for zz in range(4) for mm in range(M) for cc in range(2) for ff in range(2)
-    ]
-
-    def number(zz, mm, cc, ff):
-        return (zz * (n_ctx // 4) + mm * 2 + cc) * 2 + ff
-
-    down_pieces = down_sum.reshape(columns, 2, 2, each)
-    rounds = []
-    for dz in range(2):
-        for dc in range(2):
-            piece = lax.dynamic_slice(
-                down_pieces, (0, (z + dz) % 2, (core + dc) % 2, 0), (columns, 1, 1, each)
-            ).reshape(columns, each)
-            perm = [
-                (number(zz, mm, cc, ff), number(2 * ff + (zz + dz) % 2, mm, (cc + dc) % 2, zz // 2))
-                for zz, mm, cc, ff in devices
-            ]
-            rounds.append(lax.ppermute(piece, ("ctx", "fsdp"), perm))
-    rounds = jnp.stack(rounds).reshape(2, 2, columns, each)
-    rounds = jnp.where(z % 2 == 0, rounds, rounds[::-1])
-    rounds = jnp.where(core == 0, rounds, rounds[:, ::-1])
-    down_grad = jnp.transpose(
-        rounds.reshape(2, 2, M, segment, each), (0, 2, 1, 3, 4)
-    ).reshape(FF // 2, each)
 
     qw, kw = 128 // M, 64 // M
     query_grad = heads_grad[:, :qw]
@@ -1495,10 +1445,10 @@
     return (
         output[None],
         input_grad[None],
-        gains[0],
-        gains[2, :64] + gains[2, 64:128],
-        gains[2, 128:192],
-        gains[1],
+        gains[:8].reshape(WIDTH),
+        gains[16, :64] + gains[16, 64:],
+        gains[17, :64],
+        gains[8:16].reshape(WIDTH),
         query_grad,
         key_grad,
         value_grad,

time: 296 us -> 256 us (0.86)
  Pallas kernels: 254 us -> 217 us
  other arithmetic: 11.3 us -> 8.16 us
    pallas_call x1, Pallas kernels: 111 us -> 86.8 us  [feed_forward(): pl.pallas_call(ffn_kernel, out_shape=(shape((4, BLOCK, WIDTH), bf16), sha...]
    pallas_call x1, Pallas kernels: 83.7 us -> 63.1 us  [back(): pl.pallas_call(back_kernel, out_shape=(shape(part, f32), shape(part, f32)...]
    pallas_call x1, Pallas kernels: 59.4 us -> 67.1 us  [front(): pl.pallas_call(front_kernel, out_shape=(shape((8, ROWS, WIDTH), bf16), sh...]
    unnamed x20 -> x17, local copies, waits for them, and re-layouts: 6.69 us -> 13.3 us
    reduce_sum x2 -> x0, other arithmetic: 3.63 us -> none  [the longest x1 2.14 us: local(): glu_grad = jnp.sum(glu_got.astype(f32), axis=0)]
  transfers between devices with their start and end apart: 4 -> 0, of which waited for: 0 -> 0; matrix products, arithmetic and copies ran while one was open for 3% -> 0% of each run, Pallas kernels for 29% -> 0%
where the time goes in v2:
time: 256 us; the launch traced here: 251 us
  Pallas kernels  217 us (85%)
  local copies, waits for them, and re-layouts  24.2 us (9%)
  other arithmetic  8.16 us (3%)
    pallas_call x1, Pallas kernels, feed_forward(): pl.pallas_call(ffn_kernel, out_shape=(shape((4, BLOCK, WIDTH), bf16), sha...  86.8 us
    pallas_call x1, Pallas kernels, front(): pl.pallas_call(front_kernel, out_shape=(shape((8, ROWS, WIDTH), bf16), sh...  67.1 us
    pallas_call x1, Pallas kernels, back(): pl.pallas_call(back_kernel, out_shape=(shape(part, f32), shape(part, f32)...  63.1 us
    unnamed x17, local copies, waits for them, and re-layouts  13.3 us
    another operation x4, local copies, waits for them, and re-layouts  5.79 us

profile of v2, /device:TPU:0, one launch (start us, length us, event | category | flops | bytes accessed | tf_op | source)
XLA Modules:
  0.0 250.6 jit_solution(4560590681717679274)
XLA Ops:
  0.6 0.0 copy-start
  0.7 1.3 pad_bitcast_fusion.kgain_ref
  2.0 0.7 tile.2
  2.7 0.6 broadcast_in_dim_tile.3.qgain_ref
  3.3 0.0 copy-done
  3.3 1.2 dynamic-slice_convert_fusion.6
  4.5 0.8 pad_maximum_fusion.3.wh_ref
  5.3 2.7 %convert_element_type.2.wo_hbm.wo_own = bf16[512,1024]{1,0:T(8,128)(2,1)} convert(f32[512,1024]{1,0:T(8,128)} %param.23) | non-fusion elementwise | flops 524288 | bytes 3145728 | tf_op jit(solution)/shard_map/convert_element_type | solution.py:1378
  8.1 1.8 dynamic-slice_convert_fusion.1
  9.9 1.1 pad_maximum_fusion.wd_hbm.wd_own
  11.0 2.8 %dynamic-slice_convert_fusion.3 = (bf16[512,288]{1,0:T(8,128)(2,1)S(1)}, bf16[512,288]{1,0:T(8,128)(2,1)S(1)}, bf16[512,288]{1,0:T(8,128)(2,1)S(1)}, bf16[512,288]{1,0:T(8,128)(2,1)S(1)}) fusion(f32[512,4608]{1,0:T(8,128)} %param.25, s32[]{:T(128)S(6)} %select_n.36, s32[]{:T(128)S(6)} %select_n.37, f32[512,4608]{1,0:T(8,128)} %param.24), kind=kLoop, calls=%fused_computation.4 | loop fusion | bytes 2359304 | tf_op jit(solution)/shard_map/convert.2
  13.7 1.1 pad_maximum_fusion.2.wu_hbm.wu_own
  14.8 1.1 pad_maximum_fusion.1.wg_hbm.wg_own
  15.9 67.1 %front.1 = (bf16[8,128,1024]{2,1,0:T(8,128)(2,1)}, bf16[8,128,1024]{2,1,0:T(8,128)(2,1)}, bf16[1024,256]{1,0:T(8,128)(2,1)}, bf16[512,576]{1,0:T(8,128)(2,1)}, b...) custom-call(s32[1,8]{1,0:T(1,128)} %doc_ref.3, ...), custom_call_target="tpu_custom_call" | custom-call | tf_op jit(solution)/shard_map/front/pallas_call | solution.py:484
  83.0 86.8 %feed_forward.1 = (bf16[4,256,1024]{2,1,0:T(8,128)(2,1)}, bf16[8,128,1024]{2,1,0:T(8,128)(2,1)}, f32[128,1024]{1,0:T(8,128)}, f32[128,1024]{1,0:T(8,128)}, bf16[...) custom-call(bf16[4,256,128]{2,1,0:T(8,128)(2,1)} %get-tuple-element., ...), custom_call_target="tpu_custom_call" | custom-call | tf_op jit(solution)/shard_map/feed_forward/pallas_call | solution.py:762
  169.8 63.1 %back.1 = (f32[128,1024]{1,0:T(8,128)}, f32[128,1024]{1,0:T(8,128)}, f32[24,128]{1,0:T(8,128)}, f32[512,128]{1,0:T(8,128)}, f32[512,64]{1,0:T(8,128)}, /*index=5...) custom-call(s32[1,8]{1,0:T(1,128)} %doc_ref.3, bf16[8,128,1024]{2,1,0:T(8,128)(2,1)} %get-tuple-element.53.branch_ref, ...), custom_call_target="tpu_custom_call" | custom-call | tf_op jit(solution)/shard_map/back/pallas_call | solution.py:1243
  232.9 0.0 copy-start.3
  232.9 1.4 slice_bitcast_fusion.2
  234.2 1.3 slice_bitcast_fusion
  235.5 1.7 copy.30
  237.2 1.7 copy.27
  239.0 0.0 copy-start.2
  239.0 1.3 fusion
  240.3 0.7 copy.29
  241.0 0.7 copy.28
  241.8 0.0 copy-done.3
  241.8 1.1 copy.31
  242.8 0.0 copy-start.1
  242.8 2.3 copy.32
  245.2 0.0 copy-done.2
  245.2 1.2 copy.33
  246.3 1.9 copy.36
  248.2 1.9 copy.37
  250.1 0.0 copy-done.1
  (1 shorter events, 0.0 us)
Async XLA Ops:
  0.6 2.6 %copy-start = (f32[512,1024]{1,0:T(8,128)S(1)}, f32[512,1024]{1,0:T(8,128)}, u32[]{:S(2)}) copy-start(f32[512,1024]{1,0:T(8,128)} %param.20) | copy-start | bytes 6291460
  232.9 8.9 %copy-start.3 = (f32[512,288]{1,0:T(8,128)S(1)}, f32[512,288]{1,0:T(8,128)}, u32[]{:S(2)}) copy-start(f32[512,288]{1,0:T(8,128)} %get-tuple-element.89) | copy-start | bytes 1769476
  239.0 6.2 %copy-start.2 = (f32[2304,64]{1,0:T(8,128)S(1)}, f32[2304,64]{1,0:T(8,128)}, u32[]{:S(2)}) copy-start(f32[2304,64]{1,0:T(8,128)} %get-tuple-element.91) | copy-start | bytes 1769476
  242.8 7.3 %copy-start.1 = (f32[512,1024]{1,0:T(8,128)S(1)}, f32[512,1024]{1,0:T(8,128)}, u32[]{:S(2)}) copy-start(f32[512,1024]{1,0:T(8,128)} %param.20) | copy-start | bytes 6291460
